TPU v7x, 32 devices: a whole 2x2x4 slice. The times are simulated.
32 devices in a mesh: slot: 2 (over y), ctx: 4 (over z), fsdp: 4 (over x, core).
Axes of the slice: x: 2, y: 2, z: 4, core: 2. Of those that a mesh axis runs over, the one named last changes fastest.
Arguments:
- tokens: bfloat16 [4, 2048, 1024], P('slot', ('ctx', 'fsdp')), may hold values from -6 to 6
- lengths: int32 [4], P('slot'), may hold values from 1024 to 2048, as said below
- w_qkv: bfloat16 [1024, 3072], P(('ctx', 'fsdp')), may hold values from -0.25 to 0.25
- b_qkv: bfloat16 [3072], P(('ctx', 'fsdp')), may hold values from -1.796875 to 1.796875
- w_out: bfloat16 [1024, 1024], P(('ctx', 'fsdp')), may hold values from -1.5 to 1.5
- b_out: bfloat16 [1024], P(('ctx', 'fsdp')), may hold values from -1.796875 to 1.796875
- ln1_gain: bfloat16 [1024], P(('ctx', 'fsdp')), may hold values from 0.5 to 1.5
- ln1_bias: bfloat16 [1024], P(('ctx', 'fsdp')), may hold values from -1.796875 to 1.796875
- w_up: bfloat16 [1024, 4096], P(('ctx', 'fsdp')), may hold values from -0.1875 to 0.1875
- b_up: bfloat16 [4096], P(('ctx', 'fsdp')), may hold values from -1.796875 to 1.796875
- w_down: bfloat16 [4096, 1024], P(('ctx', 'fsdp')), may hold values from -0.09375 to 0.09375
- b_down: bfloat16 [1024], P(('ctx', 'fsdp')), may hold values from -1.796875 to 1.796875
- ln2_gain: bfloat16 [1024], P(('ctx', 'fsdp')), may hold values from 0.5 to 1.5
- ln2_bias: bfloat16 [1024], P(('ctx', 'fsdp')), may hold values from -1.796875 to 1.796875
- w_proj: bfloat16 [1024, 128], P(('ctx', 'fsdp')), may hold values from -0.1875 to 0.1875
- cot_out: bfloat16 [4, 2048, 1024], P('slot', ('ctx', 'fsdp')), may hold values from -6 to 6
- cot_emb: bfloat16 [4, 2048, 128], P('slot', ('ctx', 'fsdp')), may hold values from -6 to 6
Outputs:
- layer_out: bfloat16 [4, 2048, 1024], P('slot', ('ctx', 'fsdp'))
- embeds: bfloat16 [4, 2048, 128], P('slot', ('ctx', 'fsdp'))
- input_grad: bfloat16 [4, 2048, 1024], P('slot', ('ctx', 'fsdp'))
- grad_w_qkv: float32 [1024, 3072], P(('ctx', 'fsdp'))
- grad_b_qkv: float32 [3072], P(('ctx', 'fsdp'))
- grad_w_out: float32 [1024, 1024], P(('ctx', 'fsdp'))
- grad_b_out: float32 [1024], P(('ctx', 'fsdp'))
- grad_ln1_gain: float32 [1024], P(('ctx', 'fsdp'))
- grad_ln1_bias: float32 [1024], P(('ctx', 'fsdp'))
- grad_w_up: float32 [1024, 4096], P(('ctx', 'fsdp'))
- grad_b_up: float32 [4096], P(('ctx', 'fsdp'))
- grad_w_down: float32 [4096, 1024], P(('ctx', 'fsdp'))
- grad_b_down: float32 [1024], P(('ctx', 'fsdp'))
- grad_ln2_gain: float32 [1024], P(('ctx', 'fsdp'))
- grad_ln2_bias: float32 [1024], P(('ctx', 'fsdp'))
- grad_w_proj: float32 [1024, 128], P(('ctx', 'fsdp'))
Inputs may be any that keep to these rules, and one draw needn't show every extreme that they name: Each slot holds lengths valid positions at its start; in every draw some slot is full (2048) and some slot holds exactly 1024.
All inputs are finite; a program needn't handle non-finite values.
Results may differ from a plain program's by a relative error of at most 0.018.
Values may be sent and summed in bfloat16 or wider, within the bound.
A program may use at most 192 MiB of HBM per device.

v0:
```python
from functools import partial

import jax
import jax.numpy as jnp
from jax import lax
from jax.experimental import pallas as pl
from jax.experimental.pallas import tpu as pltpu
from jax.sharding import Mesh
from jax.sharding import PartitionSpec as P

H = 16
HD = 64
LN_EPS = 1e-05
NEG_FILL = -1e30
F32 = jnp.float32
BF16 = jnp.bfloat16
GROUP = ("ctx", "x", "core")
LANE = ("ctx", "x")
SWAP = [(0, 1), (1, 0)]
VMEM_LIMIT = 60 * 1024 * 1024


def mm(left, right):
    return jnp.dot(left, right, preferred_element_type=F32)


def contract(left, right, left_dim, right_dim):
    return lax.dot_general(
        left, right, (((left_dim,), (right_dim,)), ((), ())), preferred_element_type=F32
    )


def swap_core(value):
    return lax.ppermute(value, "core", SWAP)


def swap_slot(value):
    return lax.ppermute(value, "slot", SWAP)


def pick(stacked, index, axis):
    return lax.dynamic_index_in_dim(stacked, index, axis, keepdims=False)


MESH = pl.DeviceIdType.MESH


def at_device(**where):
    names = ("slot", "ctx", "x", "core")
    return tuple(where[n] if n in where else lax.axis_index(n) for n in names)


def greet(peers):
    barrier = pltpu.get_barrier_semaphore()
    for peer in peers:
        pl.semaphore_signal(barrier, inc=1, device_id=peer, device_id_type=MESH)
    pl.semaphore_wait(barrier, len(peers))


def group_peers(n_ctx, n_x):
    ctx, x, core = (lax.axis_index(n) for n in GROUP)
    peers = []
    for dz in range(n_ctx):
        for dx in range(n_x):
            for dc in range(2):
                if dz or dx or dc:
                    where = (lax.rem(ctx + dz, n_ctx), lax.rem(x + dx, n_x), lax.rem(core + dc, 2))
                    peers.append(where)
    return peers


def start_kernel(
    tok_ref, head_ref, small_ref, all_ref, heads_ref, smalls_ref,
    far_send, block_send, local_sem, head_recv, small_recv, block_recv, *, n_ctx, n_x
):
    part = tok_ref.shape[1]
    ctx, x, core = (lax.axis_index(n) for n in GROUP)
    me = (ctx * n_x + x) * 2 + core
    peers = group_peers(n_ctx, n_x)
    greet([at_device(ctx=z, x=a, core=c) for z, a, c in peers])

    def block_at(b):
        return all_ref.at[:, pl.ds(pl.multiple_of(b * part, part), part), :]

    pushes = []
    for k, (z, a, c) in enumerate(peers):
        them = (z * n_x + a) * 2 + c
        target = at_device(ctx=z, x=a, core=c)
        pushes.append(pltpu.make_async_remote_copy(
            head_ref.at[them], heads_ref.at[me], far_send.at[2 * k], head_recv.at[me],
            device_id=target, device_id_type=MESH))
        pushes.append(pltpu.make_async_remote_copy(
            small_ref, smalls_ref.at[me], far_send.at[2 * k + 1], small_recv.at[me],
            device_id=target, device_id_type=MESH))
    locals_ = [
        pltpu.make_async_copy(tok_ref, block_at(me), local_sem.at[0]),
        pltpu.make_async_copy(head_ref.at[me], heads_ref.at[me], local_sem.at[1]),
        pltpu.make_async_copy(small_ref, smalls_ref.at[me], local_sem.at[2]),
    ]

    def send(b, source, lane, target):
        return pltpu.make_async_remote_copy(
            source, block_at(b), block_send.at[lane, b], block_recv.at[b],
            device_id=target, device_id_type=MESH)

    up = at_device(ctx=lax.rem(ctx + 1, n_ctx))
    down = at_device(ctx=lax.rem(ctx + n_ctx - 1, n_ctx))
    side = at_device(x=1 - x)
    twin = at_device(core=1 - core)

    def here(b):
        return send(b, block_at(b), 0, twin)

    @pl.when(ctx + 1 < n_ctx)
    def _():
        send(me, tok_ref, 0, up).start()

    @pl.when(ctx > 0)
    def _():
        send(me, tok_ref, 1, down).start()

    send(me, tok_ref, 2, side).start()
    send(me, tok_ref, 3, twin).start()
    for copy in locals_:
        copy.start()

    for r in range(1, n_ctx):
        if r == n_ctx - 1:
            for push in pushes:
                push.start()
        low = ctx - r
        high = ctx + r

        @pl.when(low >= 0)
        def _():
            b = (low * n_x + x) * 2 + core
            here(b).wait_recv()

            @pl.when(ctx + 1 < n_ctx)
            def _():
                send(b, block_at(b), 0, up).start()

            send(b, block_at(b), 2, side).start()
            send(b, block_at(b), 3, twin).start()

        @pl.when(high < n_ctx)
        def _():
            b = (high * n_x + x) * 2 + core
            here(b).wait_recv()

            @pl.when(ctx > 0)
            def _():
                send(b, block_at(b), 1, down).start()

            send(b, block_at(b), 2, side).start()
            send(b, block_at(b), 3, twin).start()

    def from_side(z):
        b = (z * n_x + (1 - x)) * 2 + core
        here(b).wait_recv()
        send(b, block_at(b), 3, twin).start()

    from_side(ctx)
    for r in range(1, n_ctx):
        @pl.when(ctx - r >= 0)
        def _():
            from_side(ctx - r)

        @pl.when(ctx + r < n_ctx)
        def _():
            from_side(ctx + r)

    for z in range(n_ctx):
        for a in range(n_x):
            here((z * n_x + a) * 2 + 1 - core).wait_recv()
    for k, (z, a, c) in enumerate(peers):
        them = (z * n_x + a) * 2 + c
        pltpu.make_async_remote_copy(
            head_ref.at[them], heads_ref.at[them], far_send.at[2 * k], head_recv.at[them],
            device_id=twin, device_id_type=MESH).wait_recv()
        pltpu.make_async_remote_copy(
            small_ref, smalls_ref.at[them], far_send.at[2 * k + 1], small_recv.at[them],
            device_id=twin, device_id_type=MESH).wait_recv()
    for push in pushes:
        push.wait_send()
    for copy in locals_:
        copy.wait()

    for z in range(n_ctx):
        b = (z * n_x + x) * 2 + core

        @pl.when((z <= ctx) & (ctx + 1 < n_ctx))
        def _():
            send(b, block_at(b), 0, up).wait_send()

        @pl.when((z >= ctx) & (ctx > 0))
        def _():
            send(b, block_at(b), 1, down).wait_send()

        send(b, block_at(b), 2, side).wait_send()
        send(b, block_at(b), 3, twin).wait_send()
        other = (z * n_x + (1 - x)) * 2 + core
        send(other, block_at(other), 3, twin).wait_send()


def gather_start(tokens, heads, small):
    n_ctx, n_x = lax.axis_size("ctx"), lax.axis_size("x")
    n = 2 * n_ctx * n_x
    slots, part, width = tokens.shape
    vmem = pl.BlockSpec(memory_space=pltpu.VMEM)
    anywhere = pl.BlockSpec(memory_space=pl.ANY)
    dma = pltpu.SemaphoreType.DMA
    return pl.pallas_call(
        partial(start_kernel, n_ctx=n_ctx, n_x=n_x),
        in_specs=[vmem, vmem, vmem],
        out_specs=[anywhere, vmem, vmem],
        out_shape=[
            jax.ShapeDtypeStruct((slots, n * part, width), tokens.dtype),
            jax.ShapeDtypeStruct(heads.shape, heads.dtype),
            jax.ShapeDtypeStruct((n,) + small.shape, small.dtype),
        ],
        scratch_shapes=[
            dma((2 * (n - 1),)), dma((4, n)), dma((3,)), dma((n,)), dma((n,)), dma((n,))
        ],
        compiler_params=pltpu.CompilerParams(
            collective_id=1, has_side_effects=True, vmem_limit_bytes=VMEM_LIMIT
        ),
        cost_estimate=pl.CostEstimate(
            flops=0, bytes_accessed=2 * n * tokens.size, transcendentals=0
        ),
        name="gather_start",
    )(tokens, heads, small)


def finish_kernel(
    out_ref, small_ref, qkv_ref, red_ref, join_ref, weight_ref, one_ref,
    g_down, g_up, g_out, g_small, g_qkv, g_bias, g_in,
    pair_small, pair_qkv, sum_qkv, qkvs,
    pair_down, pair_out, last_up, joins, partial_in, pair_in,
    join_send, join_recv, far_send, qkv_recv, y_send, y_recv,
    *, n_ctx, n_x
):
    ctx, x, core = (lax.axis_index(n) for n in GROUP)
    slot = lax.axis_index("slot")
    chip = ctx * n_x + x
    me = 2 * chip + core
    shard, width = g_out.shape
    part = g_down.shape[0] // 2
    peers = group_peers(n_ctx, n_x)
    lane_peers = [(z, a) for z, a, c in peers[1::2]]
    across = at_device(slot=1 - slot)
    corner = at_device(slot=1 - slot, core=1 - core)
    twin = at_device(core=1 - core)
    greet([at_device(ctx=z, x=a, core=c) for z, a, c in peers] + [across, corner])

    def remote(source, target_ref, send_sem, recv_sem, target):
        return pltpu.make_async_remote_copy(
            source, target_ref, send_sem, recv_sem, device_id=target, device_id_type=MESH)

    started = []

    def launch(copy):
        copy.start()
        started.append(copy)
        return copy

    def pair_copy(i, source, target_ref, target):
        return launch(remote(source, target_ref, y_send.at[i], y_recv.at[i], target))

    qkv_copy = pair_copy(0, qkv_ref, pair_qkv, across)
    mine = pl.multiple_of(part + core * shard, shard)
    theirs = pl.multiple_of(part + (1 - core) * shard, shard)
    for k, (z, a) in enumerate(lane_peers):
        launch(remote(
            join_ref.at[z * n_x + a], joins.at[chip], join_send.at[k], join_recv.at[chip],
            at_device(ctx=z, x=a)))
    down_copy = pair_copy(4, red_ref.at[pl.ds(0, part)], pair_down, across)
    quarter_copies = [
        pair_copy(5, red_ref.at[pl.ds(theirs, shard)], last_up.at[0], twin),
        pair_copy(6, red_ref.at[pl.ds(mine, shard)], last_up.at[1], across),
        pair_copy(7, red_ref.at[pl.ds(theirs, shard)], last_up.at[2], corner),
    ]

    small_copy = pair_copy(1, small_ref, pair_small, across)
    out_copy = pair_copy(3, out_ref, pair_out, across)
    qkv_copy.wait_recv()
    sum_qkv[...] = (qkv_ref[...].astype(F32) + pair_qkv[...].astype(F32)).astype(BF16)
    for k, (z, a, c) in enumerate(peers):
        them = (z * n_x + a) * 2 + c
        launch(remote(
            sum_qkv.at[them], qkvs.at[me], far_send.at[k], qkv_recv.at[me],
            at_device(ctx=z, x=a, core=c)))
    qkvs[me] = sum_qkv[me]

    def add_head(source, rows_of, first):
        weight = jnp.concatenate(
            [weight_ref[b, source] for b in range(weight_ref.shape[0])], axis=0)
        for h in range(2):
            owner = core if h == 0 else 1 - core
            rows = rows_of(owner)
            cols = rows.shape[2] // 2
            rows = jnp.concatenate(
                [r for t in range(rows.shape[0]) for r in (rows[t, :, :cols], rows[t, :, cols:])],
                axis=0)
            term = contract(rows, weight, 1, 1)
            partial_in[h] = term if first else partial_in[h] + term

    add_head(chip, lambda owner: join_ref[chip, owner], True)

    half = pl.multiple_of(slot * part, part)
    other_half = pl.multiple_of((1 - slot) * part, part)
    g_down[pl.ds(half, part), :] = red_ref[pl.ds(0, part), :].astype(F32)
    down_copy.wait_recv()
    g_down[pl.ds(other_half, part), :] = pair_down[...].astype(F32)

    def place_quarter(rows, quarter_core, quarter_slot):
        for k in range(n_ctx * n_x):
            at = pl.multiple_of(((2 * k + quarter_core) * 2 + quarter_slot) * part, part)
            g_up[:, pl.ds(at, part)] = rows[:, k * part : (k + 1) * part].astype(F32)

    place_quarter(red_ref[pl.ds(mine, shard), :], core, slot)
    quarter_copies[0].wait_recv()
    place_quarter(last_up[0], 1 - core, slot)
    quarter_copies[1].wait_recv()
    place_quarter(last_up[1], core, 1 - slot)
    quarter_copies[2].wait_recv()
    place_quarter(last_up[2], 1 - core, 1 - slot)

    @pl.loop(1, n_ctx * n_x)
    def _(o):
        source = lax.rem(ctx + o // n_x, n_ctx) * n_x + lax.rem(x + o % n_x, n_x)
        remote(
            join_ref.at[source], joins.at[source], join_send.at[0], join_recv.at[source], twin
        ).wait_recv()
        add_head(source, lambda owner: joins[source, owner], False)

    in_copy = pair_copy(2, partial_in.at[1], pair_in, twin)

    small_copy.wait_recv()
    g_small[...] = small_ref[...].astype(F32) + pair_small[...].astype(F32)
    in_copy.wait_recv()
    g_in[...] = (partial_in[0] + pair_in[...] + one_ref[...]).astype(BF16)
    for z, a, c in peers:
        them = (z * n_x + a) * 2 + c
        remote(
            sum_qkv.at[them], qkvs.at[them], far_send.at[0], qkv_recv.at[them], twin
        ).wait_recv()
    for k in range(n_ctx * n_x):
        heads = [qkvs[2 * k + c, :shard, :].astype(F32) for c in range(2)]
        for t in range(3):
            at = t * width + 2 * HD * k
            g_qkv[:, at : at + 2 * HD] = jnp.concatenate(
                [h[:, t * HD : (t + 1) * HD] for h in heads], axis=1)
        for c in range(2):
            g_bias[2 * k + c : 2 * k + c + 1, :] = qkvs[2 * k + c, shard : shard + 1, :].astype(F32)
    out_copy.wait_recv()
    g_out[...] = out_ref[...].astype(F32) + pair_out[...].astype(F32)
    for copy in started:
        copy.wait_send()


def finish_grads(out, small, qkv, reduced, joined, weight, grad_one):
    n_ctx, n_x = lax.axis_size("ctx"), lax.axis_size("x")
    n = 2 * n_ctx * n_x
    shard, width = out.shape
    part = reduced.shape[0] // 2
    vmem = pl.BlockSpec(memory_space=pltpu.VMEM)
    dma = pltpu.SemaphoreType.DMA

    def low(*shape):
        return pltpu.VMEM(shape, BF16)

    def wide(*shape):
        return jax.ShapeDtypeStruct(shape, F32)

    return pl.pallas_call(
        partial(finish_kernel, n_ctx=n_ctx, n_x=n_x),
        in_specs=[vmem] * 7,
        out_specs=[vmem] * 7,
        out_shape=[
            wide(2 * part, width),
            wide(shard, 4 * width),
            wide(shard, width),
            wide(*small.shape),
            wide(shard, 3 * width),
            wide(n, qkv.shape[2]),
            jax.ShapeDtypeStruct(grad_one.shape, BF16),
        ],
        scratch_shapes=[
            low(*small.shape),
            low(*qkv.shape),
            low(*qkv.shape),
            low(*qkv.shape),
            low(part, width),
            low(*out.shape),
            low(3, shard, width),
            low(*joined.shape),
            pltpu.VMEM((2,) + grad_one.shape, F32),
            pltpu.VMEM(grad_one.shape, F32),
            dma((n_ctx * n_x - 1,)),
            dma((n_ctx * n_x,)),
            dma((n - 1,)),
            dma((n,)),
            dma((8,)),
            dma((8,)),
        ],
        compiler_params=pltpu.CompilerParams(
            collective_id=2, has_side_effects=True, vmem_limit_bytes=VMEM_LIMIT
        ),
        cost_estimate=pl.CostEstimate(flops=0, bytes_accessed=16 * joined.size, transcendentals=0),
        name="finish_grads",
    )(out, small, qkv, reduced, joined, weight, grad_one)


def lane_gather(mine_ref, all_ref, send_sem, recv_sem, local_sem, n_ctx, n_x):
    ctx, x = lax.axis_index("ctx"), lax.axis_index("x")
    chip = ctx * n_x + x
    routes = (
        at_device(ctx=lax.rem(ctx + 1, n_ctx)),
        at_device(ctx=lax.rem(ctx + n_ctx - 1, n_ctx)),
        at_device(x=1 - x),
    )

    def send(k, lane, own=False):
        return pltpu.make_async_remote_copy(
            mine_ref if own else all_ref.at[k], all_ref.at[k], send_sem.at[lane, k], recv_sem.at[k],
            device_id=routes[lane], device_id_type=MESH)

    local = pltpu.make_async_copy(mine_ref, all_ref.at[chip], local_sem)

    def begin():
        @pl.when(ctx + 1 < n_ctx)
        def _():
            send(chip, 0, own=True).start()

        @pl.when(ctx > 0)
        def _():
            send(chip, 1, own=True).start()

        send(chip, 2, own=True).start()
        local.start()

    def relay(r):
        for sign, lane, more in ((-1, 0, ctx + 1 < n_ctx), (1, 1, ctx > 0)):
            z = ctx + sign * r

            @pl.when((z >= 0) & (z < n_ctx))
            def _():
                k = z * n_x + x
                send(k, 0).wait_recv()

                @pl.when(more)
                def _():
                    send(k, lane).start()

                send(k, 2).start()

    def end():
        for z in range(n_ctx):
            k = z * n_x + x
            send(z * n_x + 1 - x, 0).wait_recv()

            @pl.when((z <= ctx) & (ctx + 1 < n_ctx))
            def _():
                send(k, 0).wait_send()

            @pl.when((z >= ctx) & (ctx > 0))
            def _():
                send(k, 1).wait_send()

            send(k, 2).wait_send()
        local.wait()

    return begin, relay, end


QB = 512
KB = 512


def turn(pair, cosine, sine):
    half = HD // 2
    lanes = lax.broadcasted_iota(jnp.int32, (1, 2 * HD), 1)
    low = lax.rem(lanes, HD) < half
    swapped = jnp.where(low, pltpu.roll(pair, 2 * HD - half, 1), pltpu.roll(pair, half, 1))
    return pair * cosine + swapped * jnp.where(low, -sine, sine)


def heads_kernel(
    len_ref, tok_ref, w_ref, b_ref, cos_ref, sin_ref, wa_ref, wu_ref, wd_ref,
    q_ref, k_ref, v_ref, mix_ref, send_ref, norm_ref, fa_ref, fu_ref, fd_ref,
    a_send, a_recv, u_send, u_recv, d_send, d_recv, local_sem, *, n_ctx, n_x, part
):
    core = lax.axis_index("core")
    ctx, x = lax.axis_index("ctx"), lax.axis_index("x")
    greet([
        at_device(x=1 - x),
        at_device(ctx=lax.rem(ctx + 1, n_ctx)),
        at_device(ctx=lax.rem(ctx + n_ctx - 1, n_ctx)),
    ])
    flows = [
        lane_gather(wa_ref, fa_ref, a_send, a_recv, local_sem.at[0], n_ctx, n_x),
        lane_gather(wu_ref, fu_ref, u_send, u_recv, local_sem.at[1], n_ctx, n_x),
        lane_gather(wd_ref, fd_ref, d_send, d_recv, local_sem.at[2], n_ctx, n_x),
    ]
    for begin, _, _ in flows:
        begin()
    slots, seq, _ = q_ref.shape

    def relay(r):
        if r < n_ctx:
            for _, hop, _ in flows:
                hop(r)

    blocks = seq // QB

    def project():
        @pl.loop(0, slots * blocks)
        def _(n):
            s, i = n // blocks, lax.rem(n, blocks)
            rows = pl.ds(pl.multiple_of(i * QB, QB), QB)
            tokens = tok_ref[pl.ds(pl.multiple_of(n * QB, QB), QB), :]
            joined = mm(tokens, w_ref[...]) + b_ref[...]
            turned = turn(joined[:, : 2 * HD], cos_ref[rows, :], sin_ref[rows, :])
            q_ref[s, rows, :] = (turned[:, :HD].astype(BF16) * HD ** (-0.5)).astype(BF16)
            k_ref[s, rows, :] = turned[:, HD:].astype(BF16)
            v_ref[s, rows, :] = joined[:, 2 * HD :].astype(BF16)

    def attend():
        @pl.loop(0, slots * blocks)
        def _(n):
            s, i = n // blocks, lax.rem(n, blocks)
            length = len_ref[s]
            rows = pl.ds(pl.multiple_of(i * QB, QB), QB)
            queries = q_ref[s, rows, :]

            @pl.when(n == blocks)
            def _():
                relay(2)

            def step(j, state):
                highest, total, mix = state
                start = pl.multiple_of(j * KB, KB)
                scores = contract(queries, k_ref[s, pl.ds(start, KB), :], 1, 1)
                ids = start + lax.broadcasted_iota(jnp.int32, (1, KB), 1)
                scores = jnp.where(ids < length, scores, NEG_FILL)
                higher = jnp.maximum(highest, jnp.max(scores, axis=1, keepdims=True))
                fade = jnp.exp(highest - higher)
                weights = jnp.exp(scores - higher)
                total = total * fade + jnp.sum(weights, axis=1, keepdims=True)
                mix = mix * fade + mm(weights.astype(BF16), v_ref[s, pl.ds(start, KB), :])
                return higher, total, mix

            highest, total, mix = lax.fori_loop(
                0,
                seq // KB,
                step,
                (
                    jnp.full((QB, 1), NEG_FILL, F32),
                    jnp.zeros((QB, 1), F32),
                    jnp.zeros((QB, HD), F32),
                ),
            )
            mix = mix / total
            mix_ref[s, rows, :] = mix
            log_norm = jnp.broadcast_to(highest + jnp.log(total), (QB, 128))
            norm_ref[s, :, rows] = jnp.transpose(log_norm)[0:1, :]
            low = mix.astype(BF16)
            chips = QB // (2 * part)
            for chip in range(chips):
                for half in range(2):
                    at = (2 * chip + half) * part
                    send_ref[i * chips + chip, half ^ core, s] = low[at : at + part]

    project()
    relay(1)
    attend()
    for r in range(3, n_ctx):
        relay(r)
    for _, _, end in flows:
        end()


def heads(lengths, tokens, weight, bias, cosine, sine, part, *shards):
    n_ctx, n_x = lax.axis_size("ctx"), lax.axis_size("x")
    chips = n_ctx * n_x
    slots, seq = lengths.shape[0], cosine.shape[0]
    vmem = pl.BlockSpec(memory_space=pltpu.VMEM)
    anywhere = pl.BlockSpec(memory_space=pl.ANY)
    dma = pltpu.SemaphoreType.DMA
    head = jax.ShapeDtypeStruct((slots, seq, HD), BF16)
    return pl.pallas_call(
        partial(heads_kernel, n_ctx=n_ctx, n_x=n_x, part=part),
        in_specs=[pl.BlockSpec(memory_space=pltpu.SMEM)] + [vmem] * 8,
        out_specs=[vmem] * 6 + [anywhere] * 3,
        out_shape=[
            head,
            head,
            head,
            jax.ShapeDtypeStruct((slots, seq, HD), F32),
            jax.ShapeDtypeStruct((chips, 2, slots, part, HD), BF16),
            jax.ShapeDtypeStruct((slots, 1, seq), F32),
        ]
        + [jax.ShapeDtypeStruct((chips,) + w.shape, w.dtype) for w in shards],
        scratch_shapes=[dma((3, chips)), dma((chips,))] * 3 + [dma((3,))],
        compiler_params=pltpu.CompilerParams(
            collective_id=5, has_side_effects=True, vmem_limit_bytes=VMEM_LIMIT
        ),
        cost_estimate=pl.CostEstimate(
            flops=16 * slots * seq * seq * HD,
            bytes_accessed=2 * tokens.size,
            transcendentals=slots * seq * seq,
        ),
        name="heads",
    )(lengths, tokens, weight, bias, cosine, sine, *shards)


def grads_kernel(
    len_ref, q_ref, k_ref, v_ref, g_ref, norm_ref, dot_ref, tok_ref, cos_ref, sin_ref,
    down_ref, up_ref, out_ref, small_ref,
    join_ref, grad_ref, red_ref, sum_ref, small_sum,
    dqt, key_grads, value_grads, total, bias, x_down, x_up, x_out, s_down, s_up, s_out,
    z_down, z_up, z_out, top_down, top_up, top_out, own_down, own_up, own_out, smalls,
    x_send, x_recv, z_send, z_recv, top_recv, small_send, small_recv, *, n_ctx, n_x, part
):
    ctx, x, core = (lax.axis_index(n) for n in GROUP)
    me = (ctx * n_x + x) * 2 + core
    peers = group_peers(n_ctx, n_x)
    greet([at_device(ctx=z, x=a, core=c) for z, a, c in peers])
    side = at_device(x=1 - x)
    arrays = (
        (down_ref, x_down, s_down, z_down, top_down, own_down),
        (up_ref, x_up, s_up, z_up, top_up, own_up),
        (out_ref, x_out, s_out, z_out, top_out, own_out),
    )

    def remote(source, target_ref, send_sem, recv_sem, target):
        return pltpu.make_async_remote_copy(
            source, target_ref, send_sem, recv_sem, device_id=target, device_id_type=MESH)

    orders = [
        sorted(range(n_ctx), key=lambda p, z=z: (p == z, -abs(p - z), -p)) for z in range(n_ctx)
    ]
    places = [
        sum(jnp.where(ctx == z, orders[z][j], 0) for z in range(n_ctx)) for j in range(n_ctx)
    ]
    above = at_device(ctx=lax.rem(ctx + 1, n_ctx))
    below = at_device(ctx=lax.rem(ctx + n_ctx - 1, n_ctx))
    first = [
        [
            remote(
                ref.at[places[j] * n_x + 1 - x], x_in.at[j], x_send.at[i, j], x_recv.at[i, j], side)
            for i, (ref, x_in, _, _, _, _) in enumerate(arrays)
        ]
        for j in range(n_ctx)
    ]

    def hop(j, i, target, last=False):
        _, _, s_low, z_in, top, _ = arrays[i]
        p = places[j]
        return remote(
            s_low.at[min(j, n_ctx - 2)], top if last else z_in.at[p], z_send.at[i, min(j, n_ctx - 2)],
            top_recv.at[i] if last else z_recv.at[i, p], target)

    pushes = []
    for k, (z, a, c) in enumerate(peers):
        them = (z * n_x + a) * 2 + c
        pushes.append(remote(
            small_ref.at[them], smalls.at[me], small_send.at[k], small_recv.at[me],
            at_device(ctx=z, x=a, core=c)))
    for copies in first:
        for copy in copies:
            copy.start()
    for copy in pushes:
        copy.start()
    smalls[me] = small_ref[me]

    def stage(j):
        p = places[j]
        going_up = p > ctx
        for i, (ref, x_in, s_low, z_in, _, own) in enumerate(arrays):
            first[j][i].wait_recv()
            own[...] = ref[p * n_x + x].astype(F32) + x_in[j].astype(F32)
            if j == n_ctx - 1:
                continue

            @pl.when((going_up & (ctx > 0)) | ((p < ctx) & (ctx < n_ctx - 1)))
            def _():
                hop(j, i, above).wait_recv()
                own[...] += z_in[p].astype(F32)

            s_low[j] = own[...].astype(BF16)

            @pl.when(going_up)
            def _():
                hop(j, i, above).start()

            @pl.when(p < ctx - 1)
            def _():
                hop(j, i, below).start()

            @pl.when(p == ctx - 1)
            def _():
                hop(j, i, below, last=True).start()

    slots, seq, _ = q_ref.shape
    total[...] = jnp.zeros_like(total)
    bias[...] = jnp.zeros_like(bias)

    def attention(s, between):
        length = len_ref[s]
        dqt[...] = jnp.zeros_like(dqt)

        @pl.loop(0, seq // KB)
        def _(j):
            start = pl.multiple_of(j * KB, KB)
            key_block = k_ref[s, pl.ds(start, KB), :]
            value_block = v_ref[s, pl.ds(start, KB), :]
            turned = jnp.transpose(key_block.astype(F32)).astype(BF16)
            ids = start + lax.broadcasted_iota(jnp.int32, (KB, 1), 0)
            shift = jnp.where(ids < length, 0.0, NEG_FILL)
            for at_step, number in between:
                @pl.when(j == at_step)
                def _():
                    stage(number)

            def step(i, state):
                key_grad, value_grad = state
                at = pl.multiple_of(i * QB, QB)
                queries = q_ref[s, pl.ds(at, QB), :]
                grads = g_ref[s, pl.ds(at, QB), :]
                scores = contract(key_block, queries, 1, 1) + shift
                probs = jnp.exp(scores - norm_ref[s, :, pl.ds(at, QB)])
                grad_probs = contract(value_block, grads, 1, 1)
                grad_scores = (probs * (grad_probs - dot_ref[s, :, pl.ds(at, QB)])).astype(BF16)
                value_grad = value_grad + mm(probs.astype(BF16), grads)
                key_grad = key_grad + mm(grad_scores, queries)
                dqt[:, pl.ds(at, QB)] += mm(turned, grad_scores)
                return key_grad, value_grad

            zero = jnp.zeros((KB, HD), F32)
            key_grad, value_grad = lax.fori_loop(0, seq // QB, step, (zero, zero))
            key_grads[pl.ds(start, KB), :] = key_grad
            value_grads[pl.ds(start, KB), :] = value_grad

    def join(s):
        @pl.loop(0, seq // QB)
        def _(i):
            at = pl.multiple_of(i * QB, QB)
            rows = pl.ds(at, QB)
            query_grad = jnp.transpose(dqt[:, rows]) * HD ** (-0.5)
            pair = jnp.concatenate([query_grad, key_grads[rows, :]], axis=1)
            turned = turn(pair, cos_ref[rows, :], -sin_ref[rows, :])
            joined = jnp.concatenate([turned, value_grads[rows, :]], axis=1).astype(BF16)
            chips = QB // (2 * part)
            for chip in range(chips):
                for owner in range(2):
                    near = (2 * chip + owner) * part
                    upper = joined[near : near + part // 2]
                    lower = joined[near + part // 2 : near + part]
                    join_ref[i * chips + chip, owner, s] = jnp.concatenate([upper, lower], axis=1)
            tokens = tok_ref[pl.ds(pl.multiple_of(s * seq + at, QB), QB), :]
            total[...] += contract(joined, tokens, 0, 0)
            bias[...] += jnp.sum(joined.astype(F32), axis=0, keepdims=True)

    for s in range(slots):
        attention(s, [(1, 1)] if s == 1 else [])
        stage(0 if s == 0 else 2)
        join(s)
    turned_total = jnp.transpose(total[...])
    shard = turned_total.shape[0] // grad_ref.shape[0]
    extra = jnp.broadcast_to(bias[...], (grad_ref.shape[1] - shard, bias.shape[1]))
    for d in range(grad_ref.shape[0]):
        grad_ref[d, :shard] = turned_total[d * shard : (d + 1) * shard].astype(BF16)
        grad_ref[d, shard:] = extra.astype(BF16)
    for j in range(slots + 1, n_ctx):
        stage(j)
    for z, a, c in peers:
        them = (z * n_x + a) * 2 + c
        remote(
            small_ref.at[them], smalls.at[them], small_send.at[0], small_recv.at[them], side
        ).wait_recv()
    small_sum[...] = jnp.sum(smalls[...].astype(F32), axis=0).astype(BF16)
    for i, (_, _, _, z_in, top, own) in enumerate(arrays):
        @pl.when(ctx > 0)
        def _():
            hop(n_ctx - 1, i, above).wait_recv()
            own[...] += z_in[ctx].astype(F32)

        @pl.when(ctx < n_ctx - 1)
        def _():
            hop(0, i, below, last=True).wait_recv()
            own[...] += top[...].astype(F32)

    rows = own_down.shape[0]
    red_ref[:rows] = own_down[...].astype(BF16)
    red_ref[rows:] = own_up[...].astype(BF16)
    sum_ref[...] = own_out[...].astype(BF16)
    for copies in first + [pushes]:
        for copy in copies:
            copy.wait_send()
    for j in range(n_ctx - 1):
        for i in range(len(arrays)):
            hop(j, i, above).wait_send()


def grads(lengths, queries, keys, values, grad_heads, norms, dots, tokens, cosine, sine,
          down, up, out, small, part):
    n_ctx, n_x = lax.axis_size("ctx"), lax.axis_size("x")
    n = 2 * n_ctx * n_x
    slots, seq, _ = queries.shape
    width = tokens.shape[1]
    shard = width // n
    cols = 3 * HD
    vmem = pl.BlockSpec(memory_space=pltpu.VMEM)
    dma = pltpu.SemaphoreType.DMA
    parts = (down, up, out)

    def low(*dims):
        return jax.ShapeDtypeStruct(dims, BF16)

    return pl.pallas_call(
        partial(grads_kernel, n_ctx=n_ctx, n_x=n_x, part=part),
        in_specs=[pl.BlockSpec(memory_space=pltpu.SMEM)] + [vmem] * 13,
        out_specs=[vmem] * 5,
        out_shape=[
            low(seq // (2 * part), 2, slots, part // 2, 2 * cols),
            low(n, shard + 16, cols),
            low(down.shape[1] + up.shape[1], width),
            low(*out.shape[1:]),
            low(*small.shape[1:]),
        ],
        scratch_shapes=[
            pltpu.VMEM((HD, seq), F32),
            pltpu.VMEM((seq, HD), F32),
            pltpu.VMEM((seq, HD), F32),
            pltpu.VMEM((cols, width), F32),
            pltpu.VMEM((1, cols), F32),
        ]
        + [pltpu.VMEM((n_ctx,) + t.shape[1:], BF16) for t in parts]
        + [pltpu.VMEM((n_ctx - 1,) + t.shape[1:], BF16) for t in parts]
        + [pltpu.VMEM((n_ctx,) + t.shape[1:], BF16) for t in parts]
        + [pltpu.VMEM(t.shape[1:], BF16) for t in parts]
        + [pltpu.VMEM(t.shape[1:], F32) for t in parts]
        + [
            pltpu.VMEM(small.shape, BF16),
            dma((3, n_ctx)),
            dma((3, n_ctx)),
            dma((3, n_ctx - 1)),
            dma((3, n_ctx)),
            dma((3,)),
            dma((n - 1,)),
            dma((n,)),
        ],
        compiler_params=pltpu.CompilerParams(
            collective_id=6, has_side_effects=True, vmem_limit_bytes=VMEM_LIMIT
        ),
        cost_estimate=pl.CostEstimate(
            flops=40 * slots * seq * seq * HD,
            bytes_accessed=4 * tokens.size,
            transcendentals=slots * seq * seq,
        ),
        name="grads",
    )(lengths, queries, keys, values, grad_heads, norms, dots, tokens, cosine, sine,
      down, up, out, small)


def norm_forward(values, gain, shift):
    center = values - jnp.mean(values, axis=-1, keepdims=True)
    spread = jnp.mean(center * center, axis=-1, keepdims=True)
    root = lax.rsqrt(spread + LN_EPS)
    unit = center * root
    return unit * gain + shift, unit, root


def norm_backward(grad, unit, root, gain):
    scaled = grad * gain
    inner = scaled - jnp.mean(scaled, axis=-1, keepdims=True)
    inner = inner - unit * jnp.mean(scaled * unit, axis=-1, keepdims=True)
    return root * inner, jnp.sum(grad * unit, axis=0), jnp.sum(grad, axis=0)


def gelu_pair(values):
    half = 0.5 + 0.5 * lax.erf(values * 0.7071067811865476)
    bell = jnp.exp(-0.5 * values * values) * 0.3989422804014327
    return values * half, half + values * bell


def rope_rows(positions):
    halfway = HD // 2
    ladder = jnp.arange(halfway, dtype=F32) * (2.0 / HD)
    frequency = jnp.power(jnp.float32(10000.0), -ladder)
    angles = positions[:, None] * frequency[None, :]
    return jnp.cos(angles), jnp.sin(angles)


def layer_kernel(
    merged_ref, tok_ref, wo_ref, up_ref, down_ref, vec_ref, full_ref, lane_ref,
    out_ref, one_ref, gm_ref, att_ref, vecs_ref, act_out, hid_out, gdn_out, gup_out, lanes_out,
    first, first_in, hid, act, slope, gdn, gup, hidden, unit_one, two,
    roots, near, near_in, far, far_in, low_out, low_in, send_sem, recv_sem, out_sem,
    lane_send, lane_recv, *, n_ctx, n_x
):
    core, slot = lax.axis_index("core"), lax.axis_index("slot")
    twin, across = at_device(core=1 - core), at_device(slot=1 - slot)
    ctx, x = lax.axis_index("ctx"), lax.axis_index("x")
    greet([
        twin,
        across,
        at_device(x=1 - x),
        at_device(ctx=lax.rem(ctx + 1, n_ctx)),
        at_device(ctx=lax.rem(ctx + n_ctx - 1, n_ctx)),
    ])
    begin_lane, relay_lane, end_lane = lane_gather(
        lane_ref, lanes_out, lane_send, lane_recv, out_sem.at[4], n_ctx, n_x)
    begin_lane()
    rows, width = tok_ref.shape
    half = rows // 2
    tile = 256
    count = [0]
    started = []

    def launch(source, target_ref, target):
        i = count[0]
        count[0] += 1
        copy = pltpu.make_async_remote_copy(
            source, target_ref, send_sem.at[i], recv_sem.at[i],
            device_id=target, device_id_type=MESH)
        copy.start()
        started.append(copy)
        return copy

    def columns(body, n=width // tile):
        @pl.loop(0, n)
        def _(t):
            body(pl.ds(pl.multiple_of(t * tile, tile), tile))

    def chunks(body, size=64):
        @pl.loop(0, rows // size)
        def _(t):
            body(pl.ds(pl.multiple_of(t * size, size), size))

    def exchange(buf, turn, stage, product):
        halves = [
            launch(buf.at[pl.ds(h * half, half)], buf.at[pl.ds((2 + h) * rows, half)], across)
            for h in range(2)
        ]
        to_twin = launch(buf.at[pl.ds(0, rows)], buf.at[pl.ds(rows, rows)], twin)
        near_buf, far_buf = near.at[turn], far.at[turn]
        to_twin.wait_recv()
        stage(0, 2 * rows)
        product(0, 2 * rows, near_buf, 0)
        near_copy = launch(
            near_buf.at[pl.ds(rows, rows)], near_in.at[turn], twin)
        back = []
        for h in range(2):
            at = (2 + h) * rows
            halves[h].wait_recv()
            launch(
                buf.at[pl.ds(at, half)], buf.at[pl.ds(at + half, half)], twin).wait_recv()
            stage(at, rows)
            product(at, rows, far_buf, h * rows)
            i = 2 * turn + h
            launch(
                far_buf.at[pl.ds(h * rows + half, half)], far_in.at[i], twin).wait_recv()
            low_out[i] = (far_buf[pl.ds(h * rows, half), :] + far_in[i]).astype(BF16)
            back.append(launch(low_out.at[i], low_in.at[i], across))
        return near_copy, back

    def out_product(cols):
        first[:, cols] = mm(merged_ref[...], wo_ref[:, cols])

    columns(out_product)
    launch(first.at[pl.ds(rows, rows)], first_in, twin).wait_recv()

    def norm_one(at):
        values = tok_ref[at, :].astype(F32) + first[at, :] + first_in[at, :] + vec_ref[0:1, :]
        normed, unit, root = norm_forward(values, vec_ref[1:2, :], vec_ref[2:3, :])
        hidden[at, :] = normed
        unit_one[at, :] = unit
        roots[0, at, :] = jnp.broadcast_to(root, (root.shape[0], 128))
        hid[at, :] = normed.astype(BF16)

    chunks(norm_one)

    def up_stage(start, size):
        def body(cols):
            values = mm(hid[start : start + size, :], up_ref[:, cols]) + vec_ref[3:4, cols]
            active, bend = gelu_pair(values)
            act[start : start + size, cols] = active.astype(BF16)
            slope[start : start + size, cols] = bend

        columns(body)

    def down_product(start, size, target, at):
        def body(cols):
            target[at : at + size, cols] = mm(act[start : start + size, :], down_ref[:, cols])

        columns(body)

    near_copy, back = exchange(hid, 0, up_stage, down_product)
    relay_lane(1)
    out_copies = [
        pltpu.make_async_copy(hid, hid_out, out_sem.at[0]),
        pltpu.make_async_copy(act, act_out, out_sem.at[1]),
    ]
    for copy in out_copies:
        copy.start()
    vecs_ref[...] = jnp.zeros_like(vecs_ref)
    near_copy.wait_recv()

    def norm_two(at, h, local):
        downward = near[0, at, :] + near_in[0, at, :] + low_in[h, local, :].astype(F32)
        values = hidden[at, :] + downward + vec_ref[4:5, :]
        normed, unit, root = norm_forward(values, vec_ref[5:6, :], vec_ref[6:7, :])
        out_ref[at, :] = normed.astype(BF16)
        grad, gain, shift = norm_backward(full_ref[at, :], unit, root, vec_ref[5:6, :])
        two[at, :] = grad
        low = grad.astype(BF16)
        gdn[at, :] = low
        vecs_ref[5:6, :] += gain[None]
        vecs_ref[6:7, :] += shift[None]
        vecs_ref[4:5, :] += jnp.sum(low.astype(F32), axis=0, keepdims=True)

    def by_half(body, h, size=64):
        @pl.loop(0, half // size)
        def _(t):
            local = pl.multiple_of(t * size, size)
            body(pl.ds(h * half + local, size), h, pl.ds(local, size))

    for h in range(2):
        back[h].wait_recv()
        by_half(norm_two, h)

    def back_stage(start, size):
        def body(cols):
            grads = contract(gdn[start : start + size, :], down_ref[cols, :], 1, 1)
            low = (grads * slope[start : start + size, cols]).astype(BF16)
            gup[start : start + size, cols] = low
            vecs_ref[3:4, cols] += jnp.sum(low.astype(F32), axis=0, keepdims=True)

        columns(body)

    def back_product(start, size, target, at):
        def body(cols):
            target[at : at + size, cols] = contract(
                gup[start : start + size, :], up_ref[cols, :], 1, 1)

        columns(body)

    relay_lane(2)
    near_copy, back = exchange(gdn, 1, back_stage, back_product)
    for r in range(3, n_ctx):
        relay_lane(r)
    late_copies = [
        pltpu.make_async_copy(gdn, gdn_out, out_sem.at[2]),
        pltpu.make_async_copy(gup, gup_out, out_sem.at[3]),
    ]
    for copy in late_copies:
        copy.start()
    near_copy.wait_recv()

    def norm_back(at, h, local):
        grad = near[1, at, :] + near_in[1, at, :] + low_in[2 + h, local, :].astype(F32)
        grad = grad + two[at, :]
        root = roots[0, at, 0:1]
        one, gain, shift = norm_backward(grad, unit_one[at, :], root, vec_ref[1:2, :])
        one_ref[at, :] = one
        low = one.astype(BF16)
        att_ref[at, :] = low
        vecs_ref[1:2, :] += gain[None]
        vecs_ref[2:3, :] += shift[None]
        vecs_ref[0:1, :] += jnp.sum(low.astype(F32), axis=0, keepdims=True)

    for h in range(2):
        back[h].wait_recv()
        by_half(norm_back, h)
    launch(att_ref.at[pl.ds(0, rows)], att_ref.at[pl.ds(rows, rows)], twin).wait_recv()

    def merged_product(cols):
        gm_ref[:, cols] = contract(att_ref[...], wo_ref[cols, :], 1, 1).astype(BF16)

    columns(merged_product, wo_ref.shape[0] // tile)
    end_lane()
    for copy in started:
        copy.wait_send()
    for copy in out_copies + late_copies:
        copy.wait()


def layer(merged, tokens, w_out, up, down, vectors, grad_full, lane_shard):
    n_ctx, n_x = lax.axis_size("ctx"), lax.axis_size("x")
    chips = n_ctx * n_x
    rows, width = tokens.shape
    hidden = up.shape[1]
    lane = w_out.shape[0]
    vmem = pl.BlockSpec(memory_space=pltpu.VMEM)
    anywhere = pl.BlockSpec(memory_space=pl.ANY)
    dma = pltpu.SemaphoreType.DMA

    def shape(*dims, dtype=BF16):
        return jax.ShapeDtypeStruct(dims, dtype)

    def wide(*dims):
        return pltpu.VMEM(dims, F32)

    def low(*dims):
        return pltpu.VMEM(dims, BF16)

    return pl.pallas_call(
        partial(layer_kernel, n_ctx=n_ctx, n_x=n_x),
        in_specs=[vmem] * 8,
        out_specs=[vmem] * 5 + [anywhere] * 5,
        out_shape=[
            shape(rows, width),
            shape(rows, width, dtype=F32),
            shape(2 * rows, lane),
            shape(2 * rows, width),
            shape(8, width, dtype=F32),
            shape(4 * rows, hidden),
            shape(4 * rows, width),
            shape(4 * rows, width),
            shape(4 * rows, hidden),
            shape(chips, *lane_shard.shape),
        ],
        scratch_shapes=[
            wide(2 * rows, width),
            wide(rows, width),
            low(4 * rows, width),
            low(4 * rows, hidden),
            wide(4 * rows, hidden),
            low(4 * rows, width),
            low(4 * rows, hidden),
            wide(rows, width),
            wide(rows, width),
            wide(rows, width),
            wide(1, rows, 128),
            wide(2, 2 * rows, width),
            wide(2, rows, width),
            wide(2, 2 * rows, width),
            wide(4, rows // 2, width),
            low(4, rows // 2, width),
            low(4, rows // 2, width),
            dma((24,)),
            dma((24,)),
            dma((5,)),
            dma((3, chips)),
            dma((chips,)),
        ],
        compiler_params=pltpu.CompilerParams(
            collective_id=3, has_side_effects=True, vmem_limit_bytes=VMEM_LIMIT
        ),
        cost_estimate=pl.CostEstimate(
            flops=16 * rows * width * hidden, bytes_accessed=16 * rows * width, transcendentals=0
        ),
        name="layer",
    )(merged, tokens, w_out, up, down, vectors, grad_full, lane_shard)


def head_device(
    tokens,
    lengths,
    w_qkv,
    b_qkv,
    w_out,
    b_out,
    ln1_gain,
    ln1_bias,
    w_up,
    b_up,
    w_down,
    b_down,
    ln2_gain,
    ln2_bias,
    w_proj,
    cot_out,
    cot_emb,
):
    n_lane = lax.axis_size("ctx") * lax.axis_size("x")
    n_group = 2 * n_lane
    core = lax.axis_index("core")
    slot = lax.axis_index("slot")
    chip = lax.axis_index("ctx") * lax.axis_size("x") + lax.axis_index("x")
    me = 2 * chip + core
    slots, part, width = tokens.shape
    seq = part * n_group
    rows = slots * part
    shard = width // n_group
    ff_shard = w_down.shape[0]
    ff_half = ff_shard // 2
    proj = w_proj.shape[1]
    head_cols = 3 * HD

    small = jnp.concatenate(
        [b_qkv, b_out, ln1_gain, ln1_bias, b_up, b_down, ln2_gain, ln2_bias]
    )
    small_at = [0]
    for piece in (b_qkv, b_out, ln1_gain, ln1_bias, b_up, b_down, ln2_gain, ln2_bias):
        small_at.append(small_at[-1] + piece.shape[0])
    small_rows = -(-small.shape[0] // proj)
    small_rows = -(-small_rows // 16) * 16
    small = jnp.pad(small, (0, small_rows * proj - small.shape[0])).reshape(small_rows, proj)
    def two_lanes(mine, theirs):
        low_first = jnp.stack([mine, theirs], axis=0)
        high_first = jnp.stack([theirs, mine], axis=0)
        return jnp.where(core == 0, low_first, high_first)

    up_split = w_up.reshape(shard, n_lane, 2, 2, ff_half)
    up_mine = pick(up_split, core, 2)
    up_theirs = swap_core(pick(up_split, 1 - core, 2))
    up_chip = two_lanes(pick(up_mine, slot, 2), pick(up_theirs, slot, 2))
    down_split = w_down.reshape(2, ff_half, width)

    by_head = w_qkv.reshape(shard, 3, n_group, HD).transpose(2, 0, 1, 3)
    all_tokens, my_head, packed = gather_start(
        tokens,
        by_head.reshape(n_group, shard, head_cols),
        jnp.concatenate([w_proj, small], axis=0),
    )
    proj_full = packed[:, :shard].reshape(width, proj)
    smalls = packed[:, shard:].reshape(n_group, small_rows * proj).astype(F32)
    qkv_bias, out_bias, gain_one, shift_one, up_bias, down_bias, gain_two, shift_two = (
        smalls[:, a:b].reshape(-1) for a, b in zip(small_at[:-1], small_at[1:])
    )

    head_weight = my_head.reshape(width, head_cols)
    all_tokens = all_tokens.reshape(slots * seq, width)
    head_bias = pick(qkv_bias.reshape(1, 3, n_group, HD), me, 2).reshape(1, head_cols)
    cosine, sine = rope_rows(jnp.arange(seq, dtype=jnp.int32).astype(F32))
    cos_wide = jnp.tile(cosine, (1, 4))
    sin_wide = jnp.tile(sine, (1, 4))
    queries, keys, values, mixture, send, norms, out_lane, up, down = heads(
        lengths,
        all_tokens,
        head_weight,
        head_bias,
        cos_wide,
        sin_wide,
        part,
        w_out,
        up_chip.reshape(2 * shard, n_lane * ff_half),
        pick(down_split, slot, 0),
    )
    out_lane, up, down = (t.reshape(-1, t.shape[2]) for t in (out_lane, up, down))
    bias_lane = pick(up_bias.reshape(n_lane, 2, 2, ff_half), core, 1)
    up_bias_own = pick(bias_lane, slot, 1).reshape(-1)

    qkv_split = w_qkv.reshape(shard, 3, n_lane, 2, HD)
    qkv_mine = pick(qkv_split, core, 3)
    qkv_theirs = swap_core(pick(qkv_split, 1 - core, 3))
    qkv_chip = two_lanes(qkv_mine, qkv_theirs).transpose(3, 0, 1, 2, 4)
    qkv_chip = qkv_chip.reshape(n_lane, 2 * shard, head_cols)

    merged = lax.all_to_all(send, LANE, 0, 0, tiled=True)
    merged = merged.transpose(1, 2, 3, 0, 4).reshape(2 * rows, n_lane * HD)

    place = me * part + jnp.arange(part, dtype=jnp.int32)
    live = (place[None, :] < lengths[:, None]).reshape(rows, 1)
    grad_out = jnp.where(live, cot_out.reshape(rows, width).astype(F32), 0.0)
    grad_emb = jnp.where(live, cot_emb.reshape(rows, proj), 0)
    grad_full = grad_out + contract(grad_emb, proj_full, 1, 1)
    vectors = jnp.stack(
        [out_bias, gain_one, shift_one, up_bias_own, down_bias, gain_two, shift_two, shift_two]
    )
    (
        out_low,
        grad_one,
        grad_merged,
        grad_att,
        vector_grads,
        active,
        hidden_low,
        grad_down,
        grad_up,
        qkv_lane,
    ) = layer(
        merged, tokens.reshape(rows, width), out_lane, up, down, vectors, grad_full, qkv_chip
    )
    d_down = contract(active, grad_down, 0, 0).astype(BF16)
    d_up = contract(hidden_low, grad_up, 0, 0).astype(BF16)
    embeds = mm(out_low, proj_full).astype(BF16)
    d_proj = contract(out_low, grad_emb, 0, 0)
    (
        d_out_bias,
        d_gain_one,
        d_shift_one,
        up_bias_own_grad,
        d_down_bias,
        d_gain_two,
        d_shift_two,
    ) = (vector_grads[i] for i in range(7))
    grad_merged = grad_merged.reshape(2, slots, part, n_lane, HD).transpose(3, 0, 1, 2, 4)
    grad_heads = lax.all_to_all(grad_merged, LANE, 0, 0, tiled=True)

    def core_order(value):
        return jnp.where(core == 0, value, jnp.flip(value, axis=1))

    grad_heads = core_order(grad_heads).transpose(2, 0, 1, 3, 4).reshape(slots, seq, HD)

    d_out = contract(merged, grad_att, 0, 0).astype(BF16)

    spread = (
        (jnp.arange(2) == core)[:, None, None] & (jnp.arange(2) == slot)[None, :, None]
    ).astype(F32)
    up_bias_grad = up_bias_own_grad.reshape(n_lane, 1, 1, ff_half) * spread[None]
    vectors = (
        d_out_bias,
        d_gain_one,
        d_shift_one,
        up_bias_grad.reshape(-1),
        d_down_bias,
        d_gain_two,
        d_shift_two,
    )
    small_grad = jnp.concatenate([v.reshape(n_group, -1) for v in vectors], axis=1)
    small_cols = small_grad.shape[1]
    vec_rows = -(-small_cols // proj)
    vec_rows = -(-(shard + vec_rows) // 16) * 16 - shard
    small_grad = jnp.pad(small_grad, ((0, 0), (0, vec_rows * proj - small_cols)))
    small_grad = jnp.concatenate(
        [d_proj.reshape(n_group, shard, proj), small_grad.reshape(n_group, vec_rows, proj)], axis=1
    )
    row_dots = jnp.sum(grad_heads.astype(F32) * mixture, axis=-1).reshape(slots, 1, seq)
    joined, d_qkv, reduced, out_sum, small_sum = grads(
        lengths,
        queries,
        keys,
        values,
        grad_heads,
        norms,
        row_dots,
        all_tokens,
        cos_wide,
        sin_wide,
        d_down.reshape(n_lane, 2 * shard, width),
        d_up.reshape(n_lane, 2 * shard, width),
        d_out.reshape(n_lane, shard, width),
        small_grad.astype(BF16),
        part,
    )
    grad_w_down, grad_w_up, grad_w_out, small_sum, grad_w_qkv, bias_rows, input_grad = finish_grads(
        out_sum,
        small_sum,
        d_qkv,
        reduced,
        joined,
        qkv_lane,
        grad_one,
    )
    grad_w_proj = small_sum[:shard]
    vec_sum = small_sum[shard:].reshape(-1)
    vec_outs = []
    at = 0
    for v in vectors:
        size = v.size // n_group
        vec_outs.append(vec_sum[at : at + size])
        at += size
    (
        grad_b_out,
        grad_gain_one,
        grad_shift_one,
        grad_b_up,
        grad_b_down,
        grad_gain_two,
        grad_shift_two,
    ) = vec_outs

    qkv_bias_grad = bias_rows.reshape(n_group, 3, HD).transpose(1, 0, 2).reshape(-1)
    grad_b_qkv = lax.dynamic_slice(qkv_bias_grad, (me * b_qkv.shape[0],), (b_qkv.shape[0],))

    return (
        out_low.reshape(slots, part, width),
        embeds.reshape(slots, part, proj),
        input_grad.reshape(slots, part, width),
        grad_w_qkv,
        grad_b_qkv,
        grad_w_out,
        grad_b_out,
        grad_gain_one,
        grad_shift_one,
        grad_w_up,
        grad_b_up,
        grad_w_down,
        grad_b_down,
        grad_gain_two,
        grad_shift_two,
        grad_w_proj,
    )


def layer_norm(hidden, gain, shift):
    center = hidden - jnp.mean(hidden, axis=-1, keepdims=True)
    spread = jnp.mean(center * center, axis=-1, keepdims=True)
    return center * lax.rsqrt(spread + LN_EPS) * gain + shift


def rope_tables(positions, head_width):
    halfway = head_width // 2
    ladder = jnp.arange(halfway, dtype=jnp.float32) * (2.0 / head_width)
    frequency = jnp.power(jnp.float32(10000.0), -ladder)
    angles = positions[:, None] * frequency[None, :]
    return (jnp.cos(angles)[:, None, :], jnp.sin(angles)[:, None, :])


def rotate(values, cosine, sine_part):
    halfway = values.shape[-1] // 2
    first_half = values[..., :halfway]
    second_half = values[..., halfway:]
    return jnp.concatenate(
        [
            first_half * cosine - second_half * sine_part,
            second_half * cosine + first_half * sine_part,
        ],
        axis=-1,
    )


def block_scores(query_block, key_block, key_start, length, scale):
    scores = (
        jnp.einsum("qhd,khd->hqk", query_block, key_block, preferred_element_type=jnp.float32)
        * scale
    )
    key_ids = key_start + jnp.arange(key_block.shape[0], dtype=jnp.int32)
    return jnp.where((key_ids < length)[None, None, :], scores, NEG_FILL)


def per_device(
    tokens,
    lengths,
    w_qkv,
    b_qkv,
    w_out,
    b_out,
    ln1_gain,
    ln1_bias,
    w_up,
    b_up,
    w_down,
    b_down,
    ln2_gain,
    ln2_bias,
    w_proj,
    cot_out,
    cot_emb,
):
    n_fsdp = lax.axis_size("fsdp")
    n_ctx = lax.axis_size("ctx")
    ctx_at = lax.axis_index("ctx")
    fsdp_at = lax.axis_index("fsdp")
    groups, tok_slot, width = tokens.shape
    heads_here = H // n_fsdp
    lane_width = heads_here * HD
    span_rows = tok_slot * n_fsdp
    key_count = span_rows * n_ctx
    row_count = groups * tok_slot
    scale = HD ** (-0.5)
    query_rows = min(512, span_rows)
    key_rows = min(2048, key_count // 4)
    query_blocks = span_rows // query_rows
    key_blocks = key_count // key_rows
    key_starts = jnp.arange(key_blocks, dtype=jnp.int32) * key_rows
    qkv_full, qkv_bias, out_full, out_bias, gain_one, shift_one = (
        lax.all_gather(w_qkv, ("ctx", "fsdp"), axis=0, tiled=True),
        lax.all_gather(b_qkv, ("ctx", "fsdp"), axis=0, tiled=True),
        lax.all_gather(w_out, ("ctx", "fsdp"), axis=0, tiled=True),
        lax.all_gather(b_out, ("ctx", "fsdp"), axis=0, tiled=True),
        lax.all_gather(ln1_gain, ("ctx", "fsdp"), axis=0, tiled=True),
        lax.all_gather(ln1_bias, ("ctx", "fsdp"), axis=0, tiled=True),
    )
    token_pos = (ctx_at * n_fsdp + fsdp_at) * tok_slot + jnp.arange(tok_slot, dtype=jnp.int32)
    live_rows = (token_pos[None, :] < lengths[:, None]).reshape(row_count, 1)
    flat_tokens = tokens.reshape(row_count, width)
    joined = jnp.dot(flat_tokens, qkv_full, preferred_element_type=jnp.float32) + qkv_bias.astype(
        jnp.float32
    )
    cosine, sine_part = rope_tables(token_pos.astype(jnp.float32), HD)
    split_heads = joined.reshape(groups, tok_slot, 3, H, HD)
    rotated_query = rotate(split_heads[:, :, 0], cosine, sine_part)
    rotated_key = rotate(split_heads[:, :, 1], cosine, sine_part)
    packed = (
        jnp.stack([rotated_query, rotated_key, split_heads[:, :, 2]], axis=2)
        .astype(jnp.bfloat16)
        .reshape(groups, tok_slot, 3, n_fsdp, lane_width)
    )
    by_heads = lax.all_to_all(packed, "fsdp", split_axis=3, concat_axis=1, tiled=True)
    queries = by_heads[:, :, 0, 0]
    local_keys = by_heads[:, :, 1, 0]
    local_values = by_heads[:, :, 2, 0]
    all_keys, all_values = (
        lax.all_gather(local_keys, "ctx", axis=1, tiled=True),
        lax.all_gather(local_values, "ctx", axis=1, tiled=True),
    )

    def attend_slot(slot_item):
        slot_queries, slot_keys, slot_values, length = slot_item
        query_split = slot_queries.reshape(query_blocks, query_rows, heads_here, HD)
        key_split = slot_keys.reshape(key_blocks, key_rows, heads_here, HD)
        value_split = slot_values.reshape(key_blocks, key_rows, heads_here, HD)

        def per_query(query_block):

            def row_stats(state_pair, key_item):
                highest, running_sum = state_pair
                scores = block_scores(query_block, key_item[0], key_item[1], length, scale)
                new_high = jnp.maximum(highest, jnp.max(scores, axis=-1))
                running_sum = running_sum * jnp.exp(highest - new_high) + jnp.sum(
                    jnp.exp(scores - new_high[..., None]), axis=-1
                )
                return ((new_high, running_sum), None)

            start_state = (
                jnp.full((heads_here, query_rows), NEG_FILL, jnp.float32),
                jnp.zeros((heads_here, query_rows), jnp.float32),
            )
            highest, running_sum = lax.scan(row_stats, start_state, (key_split, key_starts))[0]
            log_norm = highest + jnp.log(running_sum)

            def weigh_values(accumulated, key_item):
                scores = block_scores(query_block, key_item[0], key_item[2], length, scale)
                weights = jnp.exp(scores - log_norm[..., None]).astype(jnp.bfloat16)
                return (
                    accumulated
                    + jnp.einsum(
                        "hqk,khd->qhd", weights, key_item[1], preferred_element_type=jnp.float32
                    ),
                    None,
                )

            mixture = lax.scan(
                weigh_values,
                jnp.zeros((query_rows, heads_here, HD), jnp.float32),
                (key_split, value_split, key_starts),
            )[0]
            return (mixture, log_norm)

        mixture, log_norm = lax.map(per_query, query_split)
        return (mixture.reshape(span_rows, lane_width), log_norm)

    mixture, log_norms = lax.map(attend_slot, (queries, all_keys, all_values, lengths))
    merged = lax.all_to_all(
        mixture.astype(jnp.bfloat16).reshape(groups, span_rows, 1, lane_width),
        "fsdp",
        split_axis=1,
        concat_axis=2,
        tiled=True,
    ).reshape(row_count, width)
    attended = jnp.dot(merged, out_full, preferred_element_type=jnp.float32) + out_bias.astype(
        jnp.float32
    )
    hidden_one, pull_one = jax.vjp(
        layer_norm,
        flat_tokens.astype(jnp.float32) + attended,
        gain_one.astype(jnp.float32),
        shift_one.astype(jnp.float32),
    )
    hidden_low = hidden_one.astype(jnp.bfloat16)
    up_full, up_bias, down_full, down_bias, gain_two, shift_two, proj_full = (
        lax.all_gather(w_up, ("ctx", "fsdp"), axis=0, tiled=True),
        lax.all_gather(b_up, ("ctx", "fsdp"), axis=0, tiled=True),
        lax.all_gather(w_down, ("ctx", "fsdp"), axis=0, tiled=True),
        lax.all_gather(b_down, ("ctx", "fsdp"), axis=0, tiled=True),
        lax.all_gather(ln2_gain, ("ctx", "fsdp"), axis=0, tiled=True),
        lax.all_gather(ln2_bias, ("ctx", "fsdp"), axis=0, tiled=True),
        lax.all_gather(w_proj, ("ctx", "fsdp"), axis=0, tiled=True),
    )
    upward = jnp.dot(hidden_low, up_full, preferred_element_type=jnp.float32) + up_bias.astype(
        jnp.float32
    )
    active_full, pull_gelu = jax.vjp(partial(jax.nn.gelu, approximate=False), upward)
    active = active_full.astype(jnp.bfloat16)
    downward = jnp.dot(active, down_full, preferred_element_type=jnp.float32) + down_bias.astype(
        jnp.float32
    )
    out_full_rows, pull_two = jax.vjp(
        layer_norm,
        hidden_one + downward,
        gain_two.astype(jnp.float32),
        shift_two.astype(jnp.float32),
    )
    out_low = out_full_rows.astype(jnp.bfloat16)
    projected = jnp.dot(out_low, proj_full, preferred_element_type=jnp.float32)
    back_qkv, back_qkv_bias, back_out, back_out_bias, back_gain_one, back_shift_one = (
        lax.all_gather(w_qkv, ("ctx", "fsdp"), axis=0, tiled=True),
        lax.all_gather(b_qkv, ("ctx", "fsdp"), axis=0, tiled=True),
        lax.all_gather(w_out, ("ctx", "fsdp"), axis=0, tiled=True),
        lax.all_gather(b_out, ("ctx", "fsdp"), axis=0, tiled=True),
        lax.all_gather(ln1_gain, ("ctx", "fsdp"), axis=0, tiled=True),
        lax.all_gather(ln1_bias, ("ctx", "fsdp"), axis=0, tiled=True),
    )
    back_up, back_up_bias, back_down, back_down_bias, back_gain_two, back_shift_two, back_proj = (
        lax.all_gather(w_up, ("ctx", "fsdp"), axis=0, tiled=True),
        lax.all_gather(b_up, ("ctx", "fsdp"), axis=0, tiled=True),
        lax.all_gather(w_down, ("ctx", "fsdp"), axis=0, tiled=True),
        lax.all_gather(b_down, ("ctx", "fsdp"), axis=0, tiled=True),
        lax.all_gather(ln2_gain, ("ctx", "fsdp"), axis=0, tiled=True),
        lax.all_gather(ln2_bias, ("ctx", "fsdp"), axis=0, tiled=True),
        lax.all_gather(w_proj, ("ctx", "fsdp"), axis=0, tiled=True),
    )
    grad_out = jnp.where(live_rows, cot_out.reshape(row_count, width).astype(jnp.float32), 0.0)
    grad_emb = jnp.where(live_rows, cot_emb.reshape(row_count, -1), 0)
    d_proj = jnp.einsum("rd,rp->dp", out_low, grad_emb, preferred_element_type=jnp.float32)
    grad_full = grad_out + jnp.einsum(
        "rp,dp->rd", grad_emb, back_proj, preferred_element_type=jnp.float32
    )
    grad_two, d_gain_two, d_shift_two = pull_two(grad_full)
    grad_down = grad_two.astype(jnp.bfloat16)
    d_down = jnp.einsum("rf,rd->fd", active, grad_down, preferred_element_type=jnp.float32)
    d_down_bias = jnp.sum(grad_down.astype(jnp.float32), axis=0)
    grad_act = jnp.einsum("rd,fd->rf", grad_down, back_down, preferred_element_type=jnp.float32)
    grad_up = pull_gelu(grad_act)[0].astype(jnp.bfloat16)
    d_up = jnp.einsum("rd,rf->df", hidden_low, grad_up, preferred_element_type=jnp.float32)
    d_up_bias = jnp.sum(grad_up.astype(jnp.float32), axis=0)
    grad_hidden = grad_two + jnp.einsum(
        "rf,df->rd", grad_up, back_up, preferred_element_type=jnp.float32
    )
    grad_one, d_gain_one, d_shift_one = pull_one(grad_hidden)
    grad_att = grad_one.astype(jnp.bfloat16)
    d_out = jnp.einsum("rd,re->de", merged, grad_att, preferred_element_type=jnp.float32)
    d_out_bias = jnp.sum(grad_att.astype(jnp.float32), axis=0)
    grad_merged = jnp.einsum(
        "re,de->rd", grad_att, back_out, preferred_element_type=jnp.float32
    ).astype(jnp.bfloat16)
    grad_heads = lax.all_to_all(
        grad_merged.reshape(groups, tok_slot, n_fsdp, lane_width),
        "fsdp",
        split_axis=2,
        concat_axis=1,
        tiled=True,
    ).reshape(groups, span_rows, lane_width)

    def attend_back(slot_item):
        slot_queries, slot_keys, slot_values, grad_mix, log_norm, length = slot_item
        query_split = slot_queries.reshape(query_blocks, query_rows, heads_here, HD)
        key_split = slot_keys.reshape(key_blocks, key_rows, heads_here, HD)
        value_split = slot_values.reshape(key_blocks, key_rows, heads_here, HD)
        grad_split = grad_mix.reshape(query_blocks, query_rows, heads_here, HD)

        def value_pass(value_total, query_item):
            query_block, grad_block, norm_block = query_item

            def value_per_key(row_dot, key_item):
                key_block, value_block, key_start = key_item
                scores = block_scores(query_block, key_block, key_start, length, scale)
                probability = jnp.exp(scores - norm_block[..., None])
                grad_probs = jnp.einsum(
                    "qhd,khd->hqk", grad_block, value_block, preferred_element_type=jnp.float32
                )
                value_part = jnp.einsum(
                    "hqk,qhd->khd",
                    probability.astype(jnp.bfloat16),
                    grad_block,
                    preferred_element_type=jnp.float32,
                )
                return (row_dot + jnp.sum(probability * grad_probs, axis=-1), value_part)

            row_dot, value_parts = lax.scan(
                value_per_key,
                jnp.zeros((heads_here, query_rows), jnp.float32),
                (key_split, value_split, key_starts),
            )
            return (value_total + value_parts.reshape(key_count, heads_here, HD), row_dot)

        value_grad, row_dots = lax.scan(
            value_pass,
            jnp.zeros((key_count, heads_here, HD), jnp.float32),
            (query_split, grad_split, log_norm),
        )

        def key_pass(key_total, query_item):
            query_block, grad_block, norm_block, dot_block = query_item

            def key_per_key(query_accum, key_item):
                key_block, value_block, key_start = key_item
                scores = block_scores(query_block, key_block, key_start, length, scale)
                probability = jnp.exp(scores - norm_block[..., None])
                grad_probs = jnp.einsum(
                    "qhd,khd->hqk", grad_block, value_block, preferred_element_type=jnp.float32
                )
                grad_scores = (probability * (grad_probs - dot_block[..., None])).astype(
                    jnp.bfloat16
                )
                query_accum = query_accum + jnp.einsum(
                    "hqk,khd->qhd", grad_scores, key_block, preferred_element_type=jnp.float32
                )
                key_part = jnp.einsum(
                    "hqk,qhd->khd", grad_scores, query_block, preferred_element_type=jnp.float32
                )
                return (query_accum, key_part)

            query_grad, key_parts = lax.scan(
                key_per_key,
                jnp.zeros((query_rows, heads_here, HD), jnp.float32),
                (key_split, value_split, key_starts),
            )
            return (key_total + key_parts.reshape(key_count, heads_here, HD), query_grad)

        key_grad, query_grads = lax.scan(
            key_pass,
            jnp.zeros((key_count, heads_here, HD), jnp.float32),
            (query_split, grad_split, log_norm, row_dots),
        )
        return (
            query_grads.reshape(span_rows, lane_width) * scale,
            key_grad.reshape(key_count, lane_width) * scale,
            value_grad.reshape(key_count, lane_width),
        )

    grad_queries, key_terms, value_terms = lax.map(
        attend_back, (queries, all_keys, all_values, grad_heads, log_norms, lengths)
    )
    grad_keys, grad_values = (
        lax.psum_scatter(
            key_terms.astype(jnp.bfloat16), "ctx", scatter_dimension=1, tiled=True
        ).astype(jnp.float32),
        lax.psum_scatter(
            value_terms.astype(jnp.bfloat16), "ctx", scatter_dimension=1, tiled=True
        ).astype(jnp.float32),
    )
    head_pos = (ctx_at * span_rows + jnp.arange(span_rows, dtype=jnp.int32)).astype(jnp.float32)
    head_cosine, head_sine = rope_tables(head_pos, HD)
    query_back = rotate(
        grad_queries.reshape(groups, span_rows, heads_here, HD), head_cosine, -head_sine
    )
    key_back = rotate(grad_keys.reshape(groups, span_rows, heads_here, HD), head_cosine, -head_sine)
    value_back = grad_values.reshape(groups, span_rows, heads_here, HD)
    grad_pack = (
        jnp.stack([query_back, key_back, value_back], axis=2)
        .astype(jnp.bfloat16)
        .reshape(groups, span_rows, 3, 1, lane_width)
    )
    grad_joined = lax.all_to_all(
        grad_pack, "fsdp", split_axis=1, concat_axis=3, tiled=True
    ).reshape(row_count, 3 * width)
    d_qkv = jnp.einsum("rd,re->de", flat_tokens, grad_joined, preferred_element_type=jnp.float32)
    d_qkv_bias = jnp.sum(grad_joined.astype(jnp.float32), axis=0)
    input_grad = (
        jnp.einsum("re,de->rd", grad_joined, back_qkv, preferred_element_type=jnp.float32)
        + grad_one
    ).astype(jnp.bfloat16)
    shards = (
        lax.psum_scatter(d_qkv, ("ctx", "fsdp"), scatter_dimension=0, tiled=True),
        lax.psum_scatter(d_qkv_bias, ("ctx", "fsdp"), scatter_dimension=0, tiled=True),
        lax.psum_scatter(d_out, ("ctx", "fsdp"), scatter_dimension=0, tiled=True),
        lax.psum_scatter(d_out_bias, ("ctx", "fsdp"), scatter_dimension=0, tiled=True),
        lax.psum_scatter(d_gain_one, ("ctx", "fsdp"), scatter_dimension=0, tiled=True),
        lax.psum_scatter(d_shift_one, ("ctx", "fsdp"), scatter_dimension=0, tiled=True),
        lax.psum_scatter(d_up, ("ctx", "fsdp"), scatter_dimension=0, tiled=True),
        lax.psum_scatter(d_up_bias, ("ctx", "fsdp"), scatter_dimension=0, tiled=True),
        lax.psum_scatter(d_down, ("ctx", "fsdp"), scatter_dimension=0, tiled=True),
        lax.psum_scatter(d_down_bias, ("ctx", "fsdp"), scatter_dimension=0, tiled=True),
        lax.psum_scatter(d_gain_two, ("ctx", "fsdp"), scatter_dimension=0, tiled=True),
        lax.psum_scatter(d_shift_two, ("ctx", "fsdp"), scatter_dimension=0, tiled=True),
        lax.psum_scatter(d_proj, ("ctx", "fsdp"), scatter_dimension=0, tiled=True),
    )
    totals = (
        lax.psum(shards[0].astype(jnp.bfloat16), "slot").astype(jnp.float32),
        lax.psum(shards[1].astype(jnp.bfloat16), "slot").astype(jnp.float32),
        lax.psum(shards[2].astype(jnp.bfloat16), "slot").astype(jnp.float32),
        lax.psum(shards[3].astype(jnp.bfloat16), "slot").astype(jnp.float32),
        lax.psum(shards[4].astype(jnp.bfloat16), "slot").astype(jnp.float32),
        lax.psum(shards[5].astype(jnp.bfloat16), "slot").astype(jnp.float32),
        lax.psum(shards[6].astype(jnp.bfloat16), "slot").astype(jnp.float32),
        lax.psum(shards[7].astype(jnp.bfloat16), "slot").astype(jnp.float32),
        lax.psum(shards[8].astype(jnp.bfloat16), "slot").astype(jnp.float32),
        lax.psum(shards[9].astype(jnp.bfloat16), "slot").astype(jnp.float32),
        lax.psum(shards[10].astype(jnp.bfloat16), "slot").astype(jnp.float32),
        lax.psum(shards[11].astype(jnp.bfloat16), "slot").astype(jnp.float32),
        lax.psum(shards[12].astype(jnp.bfloat16), "slot").astype(jnp.float32),
    )
    return (
        out_low.reshape(groups, tok_slot, width),
        projected.astype(jnp.bfloat16).reshape(groups, tok_slot, -1),
        input_grad.reshape(groups, tok_slot, width),
        totals[0],
        totals[1],
        totals[2],
        totals[3],
        totals[4],
        totals[5],
        totals[6],
        totals[7],
        totals[8],
        totals[9],
        totals[10],
        totals[11],
        totals[12],
    )


def solution(mesh):
    n_slot, n_ctx, n_fsdp = (mesh.shape[a] for a in ("slot", "ctx", "fsdp"))
    rows_axes = ("ctx", "fsdp")
    step = per_device
    if n_slot == 2 and n_fsdp % 2 == 0 and n_ctx * n_fsdp == H:
        mesh = Mesh(
            mesh.devices.reshape(n_slot, n_ctx, n_fsdp // 2, 2), ("slot", "ctx", "x", "core")
        )
        rows_axes = GROUP
        step = head_device
    in_specs = (
        P("slot", rows_axes, None),
        P("slot"),
        P(rows_axes, None),
        P(rows_axes),
        P(rows_axes, None),
        P(rows_axes),
        P(rows_axes),
        P(rows_axes),
        P(rows_axes, None),
        P(rows_axes),
        P(rows_axes, None),
        P(rows_axes),
        P(rows_axes),
        P(rows_axes),
        P(rows_axes, None),
        P("slot", rows_axes, None),
        P("slot", rows_axes, None),
    )
    out_specs = (
        P("slot", rows_axes, None),
        P("slot", rows_axes, None),
        P("slot", rows_axes, None),
        P(rows_axes, None),
        P(rows_axes),
        P(rows_axes, None),
        P(rows_axes),
        P(rows_axes),
        P(rows_axes),
        P(rows_axes, None),
        P(rows_axes),
        P(rows_axes, None),
        P(rows_axes),
        P(rows_axes),
        P(rows_axes),
        P(rows_axes, None),
    )
    return jax.shard_map(
        step, mesh=mesh, in_specs=in_specs, out_specs=out_specs, check_vma=False
    )
```

profile of v0, /device:TPU:0, one launch (start us, length us, event | category | flops | bytes accessed | tf_op | source)
XLA Modules:
  0.0 438.4 jit_solution(8203799321779919568)
XLA Ops:
  0.7 1.5 reshape.305
  2.4 0.7 copy.143
  4.2 1.6 constant_dynamic-slice_fusion.1
  6.7 0.8 copy.106
  7.5 1.1 copy.107.head_ref
  9.3 73.2 %gather_start.1 = (bf16[2,2048,1024]{2,1,0:T(8,128)(2,1)}, bf16[16,64,192]{2,1,0:T(8,128)(2,1)}, bf16[16,80,128]{2,1,0:T(8,128)(2,1)}) custom-call(bf16[2,128,1024]{2,1,0:T(8,128)(2,1)} %tok_ref.1, bf16[16,64,192]{2,1,0:T(8,128)(2,1)} %copy.107.head_ref, bf16[80,128]{1,0:T(8,128)(2,1)} %pad_maximum_fusion.1.small_ref), custom_call_target="tpu_custom_call" | custom-call | bytes 8388608 | tf_op jit(solution)/shard_map/gather_start/pallas_call | solution.py:213
  82.5 0.9 slice_convert_fusion
  83.6 0.7 dynamic-slice_bitcast_fusion.wd_ref
  84.4 1.0 multiply_sine_fusion
  85.9 1.3 copy.110.sin_ref
  87.3 1.3 copy.109.cos_ref
  89.2 0.6 reshape.304.b_ref
  89.9 0.7 stack.35.vec_ref
  90.6 0.9 dynamic-slice_bitcast_fusion.1
  91.6 0.8 copy.142
  92.3 68.3 %heads.1 = (bf16[2,2048,64]{2,1,0:T(8,128)(2,1)}, bf16[2,2048,64]{2,1,0:T(8,128)(2,1)}, bf16[2,2048,64]{2,1,0:T(8,128)(2,1)}, f32[2,2048,64]{2,1,0:T(8,128)}, bf...) custom-call(s32[2]{0:T(128)} %len_ref.3, ...), custom_call_target="tpu_custom_call" | custom-call | flops 8589934592 | bytes 8388608 | tf_op jit(solution)/shard_map/heads/pallas_call | solution.py:592
  160.6 2.4 copy.111
  163.0 3.7 all-to-all-start
  166.9 1.3 convolution_add_fusion.full_ref
  168.2 1.5 fusion
  170.2 1.4 reshape.331.lane_ref
  171.6 9.5 %all-to-all-done = bf16[8,2,2,128,64]{3,4,2,1,0:T(8,128)(2,1)S(1)} async-done(((bf16[8,2,2,128,64]{3,4,2,1,0:T(8,128)(2,1)}), bf16[8,2,2,128,64]{3,4,2,1,0:T(8,128)(2,1)S(1)}, u32[]{:S(2)}, u32[]{:S(2)}) %all-to-all-start) | async-done | bytes 524320 | tf_op jit(solution)/shard_map/all_to_all | solution.py:1254
  181.8 1.0 copy.115.merged_ref
  182.8 77.1 %layer.1 = (bf16[256,1024]{1,0:T(8,128)(2,1)}, f32[256,1024]{1,0:T(8,128)}, bf16[512,512]{1,0:T(8,128)(2,1)}, bf16[512,1024]{1,0:T(8,128)(2,1)}, f32[8,1024]{1,0...) custom-call(bf16[512,512]{1,0:T(8,128)(2,1)} %copy.115.merged_ref, ...), custom_call_target="tpu_custom_call" | custom-call | flops 4294967296 | bytes 4194304 | tf_op jit(solution)/shard_map/layer/pallas_call | solution.py:1110
  259.9 0.8 slice.97
  260.7 0.8 convert.34
  261.4 2.0 convolution_convert_fusion.4
  263.5 1.3 copy.117
  264.7 0.9 reshape.317
  266.3 3.7 all-to-all-start.1
  270.7 6.1 %convolution_convert_fusion.1 = bf16[1024,1024]{1,0:T(8,128)(2,1)} fusion(bf16[1024,1024]{1,0:T(8,128)(2,1)} %get-tuple-element.64, bf16[1024,1024]{1,0:T(8,128)(2,1)} %get-tuple-element.65), kind=kOutput, calls=%fused_computation.2 | convolution fusion | flops 2148532224 | bytes 6291456 | tf_op jit(solution)/shard_map/dot_general | solution.py:28
  276.7 0.7 pad_maximum_fusion.small_ref
  277.5 1.7 convolution_convert_fusion.2
  279.2 3.8 convolution_convert_fusion
  283.9 0.7 copy.118
  284.6 2.6 multiply_reduce_fusion
  287.9 84.6 %grads.1 = (bf16[8,2,2,64,384]{4,3,2,1,0:T(8,128)(2,1)}, bf16[16,80,192]{2,1,0:T(8,128)(2,1)}, bf16[256,1024]{1,0:T(8,128)(2,1)}, bf16[64,1024]{1,0:T(8,128)(2,1)}, bf16[80,128]{1,0:T(8,128)(2,1)}) custom-call(s32[2]{0:T(128)} %len_ref.3, bf16[2,2048,64]{2,1,0:T(8,128)(2,1)} %get-tuple-element.58.q_ref, bf16[2,2048,64]{2,1,0:T(8,128)(2,1)} %get-tuple-element.59.k_ref, ...), custom_call_target="tpu_custom_call" | custom-call | flops 21474836480 | bytes 16777216 | tf_op jit(solution)/shard_map/grads/pallas_call | solution.py:822
  372.4 54.8 %finish_grads.1 = (f32[256,1024]{1,0:T(8,128)}, f32[64,4096]{1,0:T(8,128)}, f32[64,1024]{1,0:T(8,128)}, f32[80,128]{1,0:T(8,128)}, f32[64,3072]{1,0:T(8,128)}, /...) custom-call(bf16[64,1024]{1,0:T(8,128)(2,1)} %get-tuple-element.70.out_ref, bf16[80,128]{1,0:T(8,128)(2,1)} %get-tuple-element.71.small_ref, ...), custom_call_target="tpu_custom_call" | custom-call | bytes 12582912 | tf_op jit(solution)/shard_map/finish_grads/pallas_call | solution.py:376
  427.3 0.8 slice_bitcast_fusion
  428.1 1.4 slice.109
  430.7 0.8 reshape.325
  431.6 0.6 dynamic_slice.44
  432.2 0.8 copy.153
  433.0 1.9 copy.154
  434.9 0.9 copy.155
  435.7 0.7 copy.156
  436.5 1.0 copy.157
  437.4 1.0 copy.158
  (118 shorter events, 9.7 us)
Async XLA Ops:
  0.6 82.9 %copy-start = (bf16[256,1024]{1,0:T(8,128)(2,1)S(1)}, bf16[256,1024]{1,0:T(8,128)(2,1)}, u32[]{:S(2)}) copy-start(bf16[256,1024]{1,0:T(8,128)(2,1)} %param.27) | copy-start | bytes 1572868
  0.7 2.9 copy-start.6
  2.2 1.9 copy-start.4
  3.1 87.5 %collective-permute-start = (bf16[64,8,2,128]{3,1,2,0:T(8,128)(2,1)}, bf16[64,8,2,128]{3,1,2,0:T(8,128)(2,1)}, u32[]{:S(2)}, u32[]{:S(2)}) collective-permute-start(bf16[64,8,2,128]{3,1,2,0:T(8,128)(2,1)} %bitcast.92), channel_id=1, source_target_pairs={{0,1},{1,0},{2,3},{3,2},{4,5},{5,4},{6,7},{7,6},{8,9},{9,8},{10,11... | collective-permute-start | bytes 786440 | tf_op jit(solution)/shard_map/ppermute | solution.py:34
  4.1 2.4 copy-start.15
  4.1 2.4 copy-start.16
  4.1 2.4 copy-start.17
  4.2 2.4 copy-start.18
  4.2 2.4 copy-start.19
  4.2 2.4 copy-start.20
  4.2 2.4 copy-start.21
  4.2 2.4 copy-start.22
  5.9 2.8 copy-start.14
  5.9 162.3 %collective-permute-start.1 = (bf16[64,3,8,64]{3,2,1,0:T(8,128)(2,1)S(1)}, bf16[64,3,8,64]{3,2,1,0:T(8,128)(2,1)}, u32[]{:S(2)}, u32[]{:S(2)}) collective-permute-start(bf16[64,3,8,64]{3,2,1,0:T(8,128)(2,1)S(1)} %bitcast.116), channel_id=1, source_target_pairs={{0,1},{1,0},{2,3},{3,2},{4,5},{5,4},{6,7},{7,6},{8,9},{9,8},{10,11... | collective-permute-start | bytes 589832 | tf_op jit(solution)/shard_map/ppermute | solution.py:34
  7.5 76.8 %copy-start.23 = (s32[2]{0:T(128)S(1)}, s32[2]{0:T(128)}, u32[]{:S(2)}) copy-start(s32[2]{0:T(128)} %len_ref.3) | copy-start | bytes 28
  7.5 77.9 %copy-start.5 = (bf16[64,8,2,2,128]{4,3,2,1,0:T(2,128)(2,1)S(1)}, bf16[64,8,2,2,128]{4,3,2,1,0:T(2,128)(2,1)}, u32[]{:S(2)}) copy-start(bf16[64,8,2,2,128]{4,3,2,1,0:T(2,128)(2,1)} %copy-done.4) | copy-start | bytes 1572868
  82.5 3.2 copy-start.11
  160.6 6.1 %copy-start.13 = (bf16[2,128,128]{2,1,0:T(8,128)(2,1)S(1)}, bf16[2,128,128]{2,1,0:T(8,128)(2,1)}, u32[]{:S(2)}) copy-start(bf16[2,128,128]{2,1,0:T(8,128)(2,1)} %param.33) | copy-start | bytes 196612
  160.6 6.2 %copy-start.10 = (bf16[2,128,1024]{2,1,0:T(8,128)(2,1)S(1)}, bf16[2,128,1024]{2,1,0:T(8,128)(2,1)}, u32[]{:S(2)}) copy-start(bf16[2,128,1024]{2,1,0:T(8,128)(2,1)} %param.32) | copy-start | bytes 1572868
  163.0 18.0 %all-to-all-start = ((bf16[8,2,2,128,64]{3,4,2,1,0:T(8,128)(2,1)}), bf16[8,2,2,128,64]{3,4,2,1,0:T(8,128)(2,1)S(1)}, u32[]{:S(2)}, u32[]{:S(2)}) async-start(bf16[8,2,2,128,64]{3,4,2,1,0:T(8,128)(2,1)} %copy.111), calls=%async_computation | async-start | bytes 1048576 | tf_op jit(solution)/shard_map/all_to_all | solution.py:1254
  261.4 8.7 %copy-start.2 = (bf16[256,1024]{1,0:T(8,128)(2,1)S(1)}, bf16[256,1024]{1,0:T(8,128)(2,1)}, u32[]{:S(2)}) copy-start(bf16[256,1024]{1,0:T(8,128)(2,1)} %get-tuple-element.57) | copy-start | bytes 1572868
  266.3 17.1 %all-to-all-start.1 = ((bf16[8,2,2,128,64]{3,2,1,4,0:T(2,128)(2,1)}), bf16[8,2,2,128,64]{3,2,1,4,0:T(2,128)(2,1)S(1)}, u32[]{:S(2)}, u32[]{:S(2)}) async-start(bf16[8,2,2,128,64]{3,2,1,4,0:T(2,128)(2,1)} %bitcast.25), calls=%async_computation.1 | async-start | bytes 1048576 | tf_op jit(solution)/shard_map/all_to_all | solution.py:1293
  270.6 6.8 %copy-start.24 = (bf16[512,1024]{1,0:T(8,128)(2,1)S(1)}, bf16[512,1024]{1,0:T(8,128)(2,1)}, u32[]{:S(2)}) copy-start(bf16[512,1024]{1,0:T(8,128)(2,1)} %get-tuple-element.68) | copy-start | bytes 3145732
  270.6 8.5 %copy-start.26 = (bf16[1024,1024]{1,0:T(8,128)(2,1)S(1)}, bf16[1024,1024]{1,0:T(8,128)(2,1)}, u32[]{:S(2)}) copy-start(bf16[1024,1024]{1,0:T(8,128)(2,1)} %get-tuple-element.67) | copy-start | bytes 6291460
  276.7 2.5 copy-start.25
  284.6 3.2 copy-start.3
  427.3 7.6 %copy-start.9 = (f32[64,3072]{1,0:T(8,128)S(1)}, f32[64,3072]{1,0:T(8,128)}, u32[]{:S(2)}) copy-start(f32[64,3072]{1,0:T(8,128)} %get-tuple-element.127) | copy-start | bytes 2359300
  427.3 8.5 %copy-start.12 = (f32[64,1024]{1,0:T(8,128)S(1)}, f32[64,1024]{1,0:T(8,128)}, u32[]{:S(2)}) copy-start(f32[64,1024]{1,0:T(8,128)} %get-tuple-element.129) | copy-start | bytes 786436
  432.2 4.3 copy-start.8
  434.9 2.6 copy-start.7
  435.7 2.7 copy-start.1
where the time goes:
time: 441 us; the launch traced here: 438 us
  Pallas kernels  358 us (81%)
  local copies, waits for them, and re-layouts  37 us (8%)
  matrix products  15.1 us (3%)
  waiting for transfers between devices  9.92 us (2%)
  other arithmetic  9.09 us (2%)
  starting transfers between devices  7.98 us (2%)
    pallas_call x1, Pallas kernels, grads(): pl.pallas_call(partial(grads_kernel, n_ctx=n_ctx, n_x=n_x, part=part), in...  84.6 us
    pallas_call x1, Pallas kernels, layer(): pl.pallas_call(partial(layer_kernel, n_ctx=n_ctx, n_x=n_x), in_specs=[vme...  77.1 us
    pallas_call x1, Pallas kernels, gather_start(): pl.pallas_call(partial(start_kernel, n_ctx=n_ctx, n_x=n_x), in_specs=[vme...  73.2 us
    pallas_call x1, Pallas kernels, heads(): pl.pallas_call(partial(heads_kernel, n_ctx=n_ctx, n_x=n_x, part=part), in...  68.3 us
    pallas_call x1, Pallas kernels, finish_grads(): pl.pallas_call(partial(finish_kernel, n_ctx=n_ctx, n_x=n_x), in_specs=[vm...  54.8 us
    dot_general x5, matrix products, contract(): lax.dot_general(left, right, (((left_dim,), (right_dim,)), ((), ())), pre...  13.1 us
    all_to_all x1, waiting for transfers between devices, head_device(): merged = lax.all_to_all(send, LANE, 0, 0, tiled=True)  9.46 us
  transfers between devices with their start and end apart: 4, of which 2 were waited for; matrix products, arithmetic and copies ran while one was open for 8% of the time, Pallas kernels for 32%

commit v1 on v0

--- a/solution.py
+++ b/solution.py
@@ -474,6 +474,74 @@
     return begin, relay, end
 
 
+def lane_gather_x_first(mine_ref, all_ref, send_sem, recv_sem, local_sem, n_ctx, n_x):
+    ctx, x = lax.axis_index("ctx"), lax.axis_index("x")
+    chip = ctx * n_x + x
+    pair = ctx * n_x + 1 - x
+    routes = (
+        at_device(ctx=lax.rem(ctx + 1, n_ctx)),
+        at_device(ctx=lax.rem(ctx + n_ctx - 1, n_ctx)),
+        at_device(x=1 - x),
+    )
+    ways = ((-1, 0, ctx + 1 < n_ctx), (1, 1, ctx > 0))
+
+    def send(k, lane, own=False):
+        return pltpu.make_async_remote_copy(
+            mine_ref if own else all_ref.at[k], all_ref.at[k], send_sem.at[lane, k], recv_sem.at[k],
+            device_id=routes[lane], device_id_type=MESH)
+
+    local = pltpu.make_async_copy(mine_ref, all_ref.at[chip], local_sem)
+
+    def along(k, own=False):
+        for _, lane, more in ways:
+            @pl.when(more)
+            def _():
+                send(k, lane, own).start()
+
+    def begin():
+        send(chip, 2, own=True).start()
+        along(chip, own=True)
+        local.start()
+
+    def pass_on(r, line):
+        for sign, lane, more in ways:
+            z = ctx + sign * r
+
+            @pl.when((z >= 0) & (z < n_ctx))
+            def _():
+                k = z * n_x + line
+                send(k, lane).wait_recv()
+
+                @pl.when(more)
+                def _():
+                    send(k, lane).start()
+
+    def relay(r):
+        if r == 1:
+            send(pair, 2).wait_recv()
+            along(pair)
+        else:
+            pass_on(r - 1, 1 - x)
+        pass_on(r, x)
+
+    def end():
+        pass_on(n_ctx - 1, 1 - x)
+        send(chip, 2).wait_send()
+        for z in range(n_ctx):
+            for line in range(n_x):
+                @pl.when((z <= ctx) & (ctx + 1 < n_ctx))
+                def _():
+                    send(z * n_x + line, 0).wait_send()
+
+                @pl.when((z >= ctx) & (ctx > 0))
+                def _():
+                    send(z * n_x + line, 1).wait_send()
+
+        local.wait()
+
+    return begin, relay, end
+
+
 QB = 512
 KB = 512
 
@@ -499,7 +567,7 @@
         at_device(ctx=lax.rem(ctx + n_ctx - 1, n_ctx)),
     ])
     flows = [
-        lane_gather(wa_ref, fa_ref, a_send, a_recv, local_sem.at[0], n_ctx, n_x),
+        lane_gather_x_first(wa_ref, fa_ref, a_send, a_recv, local_sem.at[0], n_ctx, n_x),
         lane_gather(wu_ref, fu_ref, u_send, u_recv, local_sem.at[1], n_ctx, n_x),
         lane_gather(wd_ref, fd_ref, d_send, d_recv, local_sem.at[2], n_ctx, n_x),
     ]
@@ -570,7 +638,9 @@
             for chip in range(chips):
                 for half in range(2):
                     at = (2 * chip + half) * part
-                    send_ref[i * chips + chip, half ^ core, s] = low[at : at + part]
+                    upper, lower = low[at : at + part // 2], low[at + part // 2 : at + part]
+                    send_ref[i * chips + chip, half ^ core, s] = jnp.concatenate(
+                        [upper, lower], axis=1)
 
     project()
     relay(1)
@@ -598,7 +668,7 @@
             head,
             head,
             jax.ShapeDtypeStruct((slots, seq, HD), F32),
-            jax.ShapeDtypeStruct((chips, 2, slots, part, HD), BF16),
+            jax.ShapeDtypeStruct((chips, 2, slots, part // 2, 2 * HD), BF16),
             jax.ShapeDtypeStruct((slots, 1, seq), F32),
         ]
         + [jax.ShapeDtypeStruct((chips,) + w.shape, w.dtype) for w in shards],
@@ -639,7 +709,7 @@
             source, target_ref, send_sem, recv_sem, device_id=target, device_id_type=MESH)
 
     orders = [
-        sorted(range(n_ctx), key=lambda p, z=z: (p == z, -abs(p - z), -p)) for z in range(n_ctx)
+        sorted(range(n_ctx), key=lambda p, z=z: (p == z, -abs(p - z), min(p, n_ctx - 1 - p))) for z in range(n_ctx)
     ]
     places = [
         sum(jnp.where(ctx == z, orders[z][j], 0) for z in range(n_ctx)) for j in range(n_ctx)
@@ -895,22 +965,29 @@
 
 
 def layer_kernel(
-    merged_ref, tok_ref, wo_ref, up_ref, down_ref, vec_ref, full_ref, lane_ref,
-    out_ref, one_ref, gm_ref, att_ref, vecs_ref, act_out, hid_out, gdn_out, gup_out, lanes_out,
+    sent_ref, tok_ref, wo_ref, up_ref, down_ref, vec_ref, full_ref, lane_ref,
+    merged_ref, out_ref, one_ref, gm_ref, att_ref, vecs_ref, act_out, hid_out, gdn_out, gup_out, lanes_out,
     first, first_in, hid, act, slope, gdn, gup, hidden, unit_one, two,
     roots, near, near_in, far, far_in, low_out, low_in, send_sem, recv_sem, out_sem,
-    lane_send, lane_recv, *, n_ctx, n_x
+    lane_send, lane_recv, heads_in, push_send, push_recv, *, n_ctx, n_x
 ):
     core, slot = lax.axis_index("core"), lax.axis_index("slot")
     twin, across = at_device(core=1 - core), at_device(slot=1 - slot)
     ctx, x = lax.axis_index("ctx"), lax.axis_index("x")
-    greet([
-        twin,
-        across,
-        at_device(x=1 - x),
-        at_device(ctx=lax.rem(ctx + 1, n_ctx)),
-        at_device(ctx=lax.rem(ctx + n_ctx - 1, n_ctx)),
-    ])
+    chip = ctx * n_x + x
+    others = [
+        (lax.rem(ctx + o // n_x, n_ctx), lax.rem(x + o % n_x, n_x)) for o in range(1, n_ctx * n_x)
+    ]
+    greet([twin, across] + [at_device(ctx=z, x=a) for z, a in others])
+    pushes = [
+        pltpu.make_async_remote_copy(
+            sent_ref.at[z * n_x + a], heads_in.at[chip], push_send.at[o], push_recv.at[chip],
+            device_id=at_device(ctx=z, x=a), device_id_type=MESH)
+        for o, (z, a) in enumerate(others)
+    ]
+    for push in pushes:
+        push.start()
+    heads_in[chip] = sent_ref[chip]
     begin_lane, relay_lane, end_lane = lane_gather(
         lane_ref, lanes_out, lane_send, lane_recv, out_sem.at[4], n_ctx, n_x)
     begin_lane()
@@ -967,6 +1044,22 @@
             back.append(launch(low_out.at[i], low_in.at[i], across))
         return near_copy, back
 
+    for o, (z, a) in enumerate(others):
+        source = z * n_x + a
+        pltpu.make_async_remote_copy(
+            sent_ref.at[source], heads_in.at[source], push_send.at[o], push_recv.at[source],
+            device_id=twin, device_id_type=MESH).wait_recv()
+    _, owners, slots, packed, pair_width = heads_in.shape
+    for k in range(0, n_ctx * n_x, 2):
+        for h in range(owners):
+            for t in range(slots):
+                left, right = heads_in[k, h, t], heads_in[k + 1, h, t]
+                for piece in range(2):
+                    at = ((h * slots + t) * 2 + piece) * packed
+                    of = slice(piece * HD, (piece + 1) * HD)
+                    merged_ref[at : at + packed, k * HD : (k + 2) * HD] = jnp.concatenate(
+                        [left[:, of], right[:, of]], axis=1)
+
     def out_product(cols):
         first[:, cols] = mm(merged_ref[...], wo_ref[:, cols])
 
@@ -1082,13 +1175,13 @@
 
     columns(merged_product, wo_ref.shape[0] // tile)
     end_lane()
-    for copy in started:
+    for copy in started + pushes:
         copy.wait_send()
     for copy in out_copies + late_copies:
         copy.wait()
 
 
-def layer(merged, tokens, w_out, up, down, vectors, grad_full, lane_shard):
+def layer(sent, tokens, w_out, up, down, vectors, grad_full, lane_shard):
     n_ctx, n_x = lax.axis_size("ctx"), lax.axis_size("x")
     chips = n_ctx * n_x
     rows, width = tokens.shape
@@ -1110,8 +1203,9 @@
     return pl.pallas_call(
         partial(layer_kernel, n_ctx=n_ctx, n_x=n_x),
         in_specs=[vmem] * 8,
-        out_specs=[vmem] * 5 + [anywhere] * 5,
+        out_specs=[vmem] * 6 + [anywhere] * 5,
         out_shape=[
+            shape(2 * rows, lane),
             shape(rows, width),
             shape(rows, width, dtype=F32),
             shape(2 * rows, lane),
@@ -1146,6 +1240,9 @@
             dma((5,)),
             dma((3, chips)),
             dma((chips,)),
+            low(*sent.shape),
+            dma((chips - 1,)),
+            dma((chips,)),
         ],
         compiler_params=pltpu.CompilerParams(
             collective_id=3, has_side_effects=True, vmem_limit_bytes=VMEM_LIMIT
@@ -1154,7 +1251,7 @@
             flops=16 * rows * width * hidden, bytes_accessed=16 * rows * width, transcendentals=0
         ),
         name="layer",
-    )(merged, tokens, w_out, up, down, vectors, grad_full, lane_shard)
+    )(sent, tokens, w_out, up, down, vectors, grad_full, lane_shard)
 
 
 def head_device(
@@ -1251,9 +1348,6 @@
     qkv_chip = two_lanes(qkv_mine, qkv_theirs).transpose(3, 0, 1, 2, 4)
     qkv_chip = qkv_chip.reshape(n_lane, 2 * shard, head_cols)
 
-    merged = lax.all_to_all(send, LANE, 0, 0, tiled=True)
-    merged = merged.transpose(1, 2, 3, 0, 4).reshape(2 * rows, n_lane * HD)
-
     place = me * part + jnp.arange(part, dtype=jnp.int32)
     live = (place[None, :] < lengths[:, None]).reshape(rows, 1)
     grad_out = jnp.where(live, cot_out.reshape(rows, width).astype(F32), 0.0)
@@ -1263,6 +1357,7 @@
         [out_bias, gain_one, shift_one, up_bias_own, down_bias, gain_two, shift_two, shift_two]
     )
     (
+        merged,
         out_low,
         grad_one,
         grad_merged,
@@ -1274,7 +1369,7 @@
         grad_up,
         qkv_lane,
     ) = layer(
-        merged, tokens.reshape(rows, width), out_lane, up, down, vectors, grad_full, qkv_chip
+        send, tokens.reshape(rows, width), out_lane, up, down, vectors, grad_full, qkv_chip
     )
     d_down = contract(active, grad_down, 0, 0).astype(BF16)
     d_up = contract(hidden_low, grad_up, 0, 0).astype(BF16)

time: 441 us -> 432 us (0.980)
  waiting for transfers between devices: 9.92 us -> 0.42 us
  Pallas kernels: 358 us -> 364 us
    pallas_call x1, Pallas kernels: 77.1 us -> 91 us  [layer(): pl.pallas_call(partial(layer_kernel, n_ctx=n_ctx, n_x=n_x), in_specs=[vme...]
    pallas_call x1, Pallas kernels: 84.6 us -> 74.8 us  [grads(): pl.pallas_call(partial(grads_kernel, n_ctx=n_ctx, n_x=n_x, part=part), in...]
    all_to_all x1 -> x0, waiting for transfers between devices: 9.46 us -> none  [head_device(): merged = lax.all_to_all(send, LANE, 0, 0, tiled=True)]
  transfers between devices with their start and end apart: 4 -> 3, of which waited for: 2 -> 1; matrix products, arithmetic and copies ran while one was open for 8% -> 8% of each run, Pallas kernels for 32% -> 17%
where the time goes in v1:
time: 432 us; the launch traced here: 429 us
  Pallas kernels  364 us (84%)
  local copies, waits for them, and re-layouts  34.7 us (8%)
  matrix products  16.2 us (4%)
  other arithmetic  9.03 us (2%)
    pallas_call x1, Pallas kernels, layer(): pl.pallas_call(partial(layer_kernel, n_ctx=n_ctx, n_x=n_x), in_specs=[vme...  91 us
    pallas_call x1, Pallas kernels, grads(): pl.pallas_call(partial(grads_kernel, n_ctx=n_ctx, n_x=n_x, part=part), in...  74.8 us
    pallas_call x1, Pallas kernels, gather_start(): pl.pallas_call(partial(start_kernel, n_ctx=n_ctx, n_x=n_x), in_specs=[vme...  73.2 us
    pallas_call x1, Pallas kernels, heads(): pl.pallas_call(partial(heads_kernel, n_ctx=n_ctx, n_x=n_x, part=part), in...  67.2 us
    pallas_call x1, Pallas kernels, finish_grads(): pl.pallas_call(partial(finish_kernel, n_ctx=n_ctx, n_x=n_x), in_specs=[vm...  57.5 us
    dot_general x5, matrix products, contract(): lax.dot_general(left, right, (((left_dim,), (right_dim,)), ((), ())), pre...  14.2 us
  transfers between devices with their start and end apart: 3, of which 1 were waited for; matrix products, arithmetic and copies ran while one was open for 8% of the time, Pallas kernels for 17%

profile of v1, /device:TPU:0, one launch (start us, length us, event | category | flops | bytes accessed | tf_op | source)
XLA Modules:
  0.0 429.5 jit_solution(7345963839178894424)
XLA Ops:
  0.7 1.5 reshape.302
  2.4 0.7 copy.117
  4.2 1.6 constant_dynamic-slice_fusion.1
  5.9 0.8 copy.114
  7.5 0.8 copy.83
  8.4 1.1 copy.84.head_ref
  10.1 73.2 %gather_start.1 = (bf16[2,2048,1024]{2,1,0:T(8,128)(2,1)}, bf16[16,64,192]{2,1,0:T(8,128)(2,1)}, bf16[16,80,128]{2,1,0:T(8,128)(2,1)}) custom-call(bf16[2,128,1024]{2,1,0:T(8,128)(2,1)} %tok_ref.1, bf16[16,64,192]{2,1,0:T(8,128)(2,1)} %copy.84.head_ref, bf16[80,128]{1,0:T(8,128)(2,1)} %pad_maximum_fusion.1.small_ref), custom_call_target="tpu_custom_call" | custom-call | bytes 8388608 | tf_op jit(solution)/shard_map/gather_start/pallas_call | solution.py:213
  83.3 0.9 slice_convert_fusion
  84.1 1.0 slice.93
  85.5 1.0 multiply_sine_fusion
  86.8 2.3 convolution_add_fusion.full_ref
  89.2 1.3 copy.87.sin_ref
  90.7 1.3 copy.86.cos_ref
  92.6 0.6 reshape.301.b_ref
  93.2 0.7 stack.35.vec_ref
  93.9 0.7 dynamic-slice_bitcast_fusion.wd_ref
  94.6 1.5 fusion
  96.6 1.5 reshape.327.lane_ref
  98.1 0.9 dynamic-slice_bitcast_fusion.1
  99.1 0.8 copy.116
  99.8 67.2 %heads.1 = (bf16[2,2048,64]{2,1,0:T(8,128)(2,1)}, bf16[2,2048,64]{2,1,0:T(8,128)(2,1)}, bf16[2,2048,64]{2,1,0:T(8,128)(2,1)}, f32[2,2048,64]{2,1,0:T(8,128)}, bf...) custom-call(s32[2]{0:T(128)} %len_ref.3, ...), custom_call_target="tpu_custom_call" | custom-call | flops 8589934592 | bytes 8388608 | tf_op jit(solution)/shard_map/heads/pallas_call | solution.py:662
  167.0 91.0 %layer.1 = (bf16[512,512]{1,0:T(8,128)(2,1)}, bf16[256,1024]{1,0:T(8,128)(2,1)}, f32[256,1024]{1,0:T(8,128)}, bf16[512,512]{1,0:T(8,128)(2,1)}, bf16[512,1024]{1...) custom-call(bf16[8,2,2,64,128]{4,3,2,1,0:T(8,128)(2,1)} %get-tuple-e, ...), custom_call_target="tpu_custom_call" | custom-call | flops 4294967296 | bytes 4194304 | tf_op jit(solution)/shard_map/layer/pallas_call | solution.py:1203
  258.1 0.8 slice.97
  258.8 0.8 convert.34
  259.6 2.0 convolution_convert_fusion.4
  261.6 1.3 copy.91
  262.9 0.9 reshape.313
  264.4 3.7 all-to-all-start
  268.8 6.1 %convolution_convert_fusion.1 = bf16[1024,1024]{1,0:T(8,128)(2,1)} fusion(bf16[1024,1024]{1,0:T(8,128)(2,1)} %get-tuple-element.65, bf16[1024,1024]{1,0:T(8,128)(2,1)} %get-tuple-element.66), kind=kOutput, calls=%fused_computation.2 | convolution fusion | flops 2148532224 | bytes 6291456 | tf_op jit(solution)/shard_map/dot_general | solution.py:28
  274.9 0.7 pad_maximum_fusion.small_ref
  275.6 1.7 convolution_convert_fusion.2
  277.4 3.8 convolution_convert_fusion
  282.1 0.7 copy.92
  282.8 2.6 multiply_reduce_fusion
  285.4 0.6 reshape.315.dot_ref
  286.0 74.8 %grads.1 = (bf16[8,2,2,64,384]{4,3,2,1,0:T(8,128)(2,1)}, bf16[16,80,192]{2,1,0:T(8,128)(2,1)}, bf16[256,1024]{1,0:T(8,128)(2,1)}, bf16[64,1024]{1,0:T(8,128)(2,1)}, bf16[80,128]{1,0:T(8,128)(2,1)}) custom-call(s32[2]{0:T(128)} %len_ref.3, bf16[2,2048,64]{2,1,0:T(8,128)(2,1)} %get-tuple-element.59.q_ref, bf16[2,2048,64]{2,1,0:T(8,128)(2,1)} %get-tuple-element.60.k_ref, ...), custom_call_target="tpu_custom_call" | custom-call | flops 21474836480 | bytes 16777216 | tf_op jit(solution)/shard_map/grads/pallas_call | solution.py:892
  360.8 57.5 %finish_grads.1 = (f32[256,1024]{1,0:T(8,128)}, f32[64,4096]{1,0:T(8,128)}, f32[64,1024]{1,0:T(8,128)}, f32[80,128]{1,0:T(8,128)}, f32[64,3072]{1,0:T(8,128)}, /...) custom-call(bf16[64,1024]{1,0:T(8,128)(2,1)} %get-tuple-element.72.out_ref, bf16[80,128]{1,0:T(8,128)(2,1)} %get-tuple-element.73.small_ref, ...), custom_call_target="tpu_custom_call" | custom-call | bytes 12582912 | tf_op jit(solution)/shard_map/finish_grads/pallas_call | solution.py:376
  418.4 0.8 slice_bitcast_fusion
  419.2 1.4 slice.109
  420.5 0.6 slice.127
  421.8 0.8 reshape.321
  422.6 0.6 dynamic_slice.44
  423.3 0.8 copy.127
  424.1 1.9 copy.128
  426.0 0.9 copy.129
  426.8 0.7 copy.130
  427.5 1.0 copy.131
  428.5 1.0 copy.132
  (110 shorter events, 7.5 us)
Async XLA Ops:
  0.6 93.2 %copy-start = (bf16[256,1024]{1,0:T(8,128)(2,1)S(1)}, bf16[256,1024]{1,0:T(8,128)(2,1)}, u32[]{:S(2)}) copy-start(bf16[256,1024]{1,0:T(8,128)(2,1)} %param.27) | copy-start | bytes 1572868
  0.7 2.9 copy-start.6
  2.2 1.9 copy-start.4
  3.1 95.0 %collective-permute-start = (bf16[64,8,2,128]{3,1,2,0:T(8,128)(2,1)}, bf16[64,8,2,128]{3,1,2,0:T(8,128)(2,1)}, u32[]{:S(2)}, u32[]{:S(2)}) collective-permute-start(bf16[64,8,2,128]{3,1,2,0:T(8,128)(2,1)} %bitcast.89), channel_id=1, source_target_pairs={{0,1},{1,0},{2,3},{3,2},{4,5},{5,4},{6,7},{7,6},{8,9},{9,8},{10,11... | collective-permute-start | bytes 786440 | tf_op jit(solution)/shard_map/ppermute | solution.py:34
  4.1 2.6 copy-start.21
  4.1 3.2 copy-start.13
  4.1 3.2 copy-start.14
  4.2 3.2 copy-start.15
  4.2 3.2 copy-start.16
  4.2 3.2 copy-start.17
  4.2 3.2 copy-start.18
  4.2 3.2 copy-start.19
  4.2 3.2 copy-start.20
  6.7 2.8 copy-start.12
  6.7 87.9 %collective-permute-start.1 = (bf16[64,3,8,64]{3,2,1,0:T(8,128)(2,1)}, bf16[64,3,8,64]{3,2,1,0:T(8,128)(2,1)}, u32[]{:S(2)}, u32[]{:S(2)}) collective-permute-start(bf16[64,3,8,64]{3,2,1,0:T(8,128)(2,1)} %bitcast.86), channel_id=1, source_target_pairs={{0,1},{1,0},{2,3},{3,2},{4,5},{5,4},{6,7},{7,6},{8,9},{9,8},{10,11... | collective-permute-start | bytes 589832 | tf_op jit(solution)/shard_map/ppermute | solution.py:34
  8.3 77.0 %copy-start.11 = (bf16[2,128,128]{2,1,0:T(8,128)(2,1)S(1)}, bf16[2,128,128]{2,1,0:T(8,128)(2,1)}, u32[]{:S(2)}) copy-start(bf16[2,128,128]{2,1,0:T(8,128)(2,1)} %param.33) | copy-start | bytes 196612
  8.4 78.1 %copy-start.5 = (bf16[64,8,2,2,128]{4,3,2,1,0:T(2,128)(2,1)S(1)}, bf16[64,8,2,2,128]{4,3,2,1,0:T(2,128)(2,1)}, u32[]{:S(2)}) copy-start(bf16[64,8,2,2,128]{4,3,2,1,0:T(2,128)(2,1)} %copy-done.4) | copy-start | bytes 1572868
  259.6 8.7 %copy-start.2 = (bf16[256,1024]{1,0:T(8,128)(2,1)S(1)}, bf16[256,1024]{1,0:T(8,128)(2,1)}, u32[]{:S(2)}) copy-start(bf16[256,1024]{1,0:T(8,128)(2,1)} %get-tuple-element.58) | copy-start | bytes 1572868
  264.4 17.1 %all-to-all-start = ((bf16[8,2,2,128,64]{3,2,1,4,0:T(2,128)(2,1)}), bf16[8,2,2,128,64]{3,2,1,4,0:T(2,128)(2,1)S(1)}, u32[]{:S(2)}, u32[]{:S(2)}) async-start(bf16[8,2,2,128,64]{3,2,1,4,0:T(2,128)(2,1)} %bitcast.24), calls=%async_computation | async-start | bytes 1048576 | tf_op jit(solution)/shard_map/all_to_all | solution.py:1388
  268.8 6.8 %copy-start.22 = (bf16[512,1024]{1,0:T(8,128)(2,1)S(1)}, bf16[512,1024]{1,0:T(8,128)(2,1)}, u32[]{:S(2)}) copy-start(bf16[512,1024]{1,0:T(8,128)(2,1)} %get-tuple-element.70) | copy-start | bytes 3145732
  268.8 6.8 %copy-start.23 = (bf16[512,512]{1,0:T(8,128)(2,1)S(1)}, bf16[512,512]{1,0:T(8,128)(2,1)}, u32[]{:S(2)}) copy-start(bf16[512,512]{1,0:T(8,128)(2,1)} %get-tuple-element.69) | copy-start | bytes 1572868
  268.8 8.6 %copy-start.25 = (bf16[1024,1024]{1,0:T(8,128)(2,1)S(1)}, bf16[1024,1024]{1,0:T(8,128)(2,1)}, u32[]{:S(2)}) copy-start(bf16[1024,1024]{1,0:T(8,128)(2,1)} %get-tuple-element.68) | copy-start | bytes 6291460
  274.9 2.5 copy-start.24
  282.8 3.2 copy-start.3
  418.4 7.6 %copy-start.9 = (f32[64,3072]{1,0:T(8,128)S(1)}, f32[64,3072]{1,0:T(8,128)}, u32[]{:S(2)}) copy-start(f32[64,3072]{1,0:T(8,128)} %get-tuple-element.129) | copy-start | bytes 2359300
  418.4 8.5 %copy-start.10 = (f32[64,1024]{1,0:T(8,128)S(1)}, f32[64,1024]{1,0:T(8,128)}, u32[]{:S(2)}) copy-start(f32[64,1024]{1,0:T(8,128)} %get-tuple-element.131) | copy-start | bytes 786436
  423.3 4.3 copy-start.8
  425.9 2.6 copy-start.7
  426.8 2.7 copy-start.1

commit v2 on v1

--- a/solution.py
+++ b/solution.py
@@ -966,10 +966,11 @@
 
 def layer_kernel(
     sent_ref, tok_ref, wo_ref, up_ref, down_ref, vec_ref, full_ref, lane_ref,
-    merged_ref, out_ref, one_ref, gm_ref, att_ref, vecs_ref, act_out, hid_out, gdn_out, gup_out, lanes_out,
+    merged_ref, out_ref, one_ref, ghead_ref, att_ref, vecs_ref, d_down_ref, d_up_ref, lanes_out,
     first, first_in, hid, act, slope, gdn, gup, hidden, unit_one, two,
     roots, near, near_in, far, far_in, low_out, low_in, send_sem, recv_sem, out_sem,
-    lane_send, lane_recv, heads_in, push_send, push_recv, *, n_ctx, n_x
+    lane_send, lane_recv, heads_in, push_send, push_recv,
+    gm, heads_out, heads_back, back_send, back_recv, *, n_ctx, n_x
 ):
     core, slot = lax.axis_index("core"), lax.axis_index("slot")
     twin, across = at_device(core=1 - core), at_device(slot=1 - slot)
@@ -989,7 +990,7 @@
         push.start()
     heads_in[chip] = sent_ref[chip]
     begin_lane, relay_lane, end_lane = lane_gather(
-        lane_ref, lanes_out, lane_send, lane_recv, out_sem.at[4], n_ctx, n_x)
+        lane_ref, lanes_out, lane_send, lane_recv, out_sem.at[0], n_ctx, n_x)
     begin_lane()
     rows, width = tok_ref.shape
     half = rows // 2
@@ -1017,7 +1018,7 @@
         def _(t):
             body(pl.ds(pl.multiple_of(t * size, size), size))
 
-    def exchange(buf, turn, stage, product):
+    def exchange(buf, turn, stage, product, between):
         halves = [
             launch(buf.at[pl.ds(h * half, half)], buf.at[pl.ds((2 + h) * rows, half)], across)
             for h in range(2)
@@ -1029,6 +1030,7 @@
         product(0, 2 * rows, near_buf, 0)
         near_copy = launch(
             near_buf.at[pl.ds(rows, rows)], near_in.at[turn], twin)
+        between()
         back = []
         for h in range(2):
             at = (2 + h) * rows
@@ -1091,14 +1093,8 @@
 
         columns(body)
 
-    near_copy, back = exchange(hid, 0, up_stage, down_product)
-    relay_lane(1)
-    out_copies = [
-        pltpu.make_async_copy(hid, hid_out, out_sem.at[0]),
-        pltpu.make_async_copy(act, act_out, out_sem.at[1]),
-    ]
-    for copy in out_copies:
-        copy.start()
+    near_copy, back = exchange(hid, 0, up_stage, down_product, lambda: relay_lane(1))
+    relay_lane(2)
     vecs_ref[...] = jnp.zeros_like(vecs_ref)
     near_copy.wait_recv()
 
@@ -1141,16 +1137,11 @@
 
         columns(body)
 
-    relay_lane(2)
-    near_copy, back = exchange(gdn, 1, back_stage, back_product)
-    for r in range(3, n_ctx):
-        relay_lane(r)
-    late_copies = [
-        pltpu.make_async_copy(gdn, gdn_out, out_sem.at[2]),
-        pltpu.make_async_copy(gup, gup_out, out_sem.at[3]),
-    ]
-    for copy in late_copies:
-        copy.start()
+    def last_relays():
+        for r in range(3, n_ctx):
+            relay_lane(r)
+
+    near_copy, back = exchange(gdn, 1, back_stage, back_product, last_relays)
     near_copy.wait_recv()
 
     def norm_back(at, h, local):
@@ -1171,14 +1162,54 @@
     launch(att_ref.at[pl.ds(0, rows)], att_ref.at[pl.ds(rows, rows)], twin).wait_recv()
 
     def merged_product(cols):
-        gm_ref[:, cols] = contract(att_ref[...], wo_ref[cols, :], 1, 1).astype(BF16)
+        gm[:, cols] = contract(att_ref[...], wo_ref[cols, :], 1, 1).astype(BF16)
 
     columns(merged_product, wo_ref.shape[0] // tile)
+    for k in range(n_ctx * n_x):
+        of = slice(k * HD, (k + 1) * HD)
+        for h in range(owners):
+            for t in range(slots):
+                at = (h * slots + t) * 2 * packed
+                heads_out[k, h, t] = jnp.concatenate(
+                    [gm[at : at + packed, of], gm[at + packed : at + 2 * packed, of]], axis=1)
+    returns = [
+        pltpu.make_async_remote_copy(
+            heads_out.at[z * n_x + a], heads_back.at[chip], back_send.at[o], back_recv.at[chip],
+            device_id=at_device(ctx=z, x=a), device_id_type=MESH)
+        for o, (z, a) in enumerate(others)
+    ]
+    for copy in returns:
+        copy.start()
+    heads_back[chip] = heads_out[chip]
+
+    half_tile = tile // 2
+
+    @pl.loop(0, width // tile)
+    def _(t):
+        cols = pl.ds(pl.multiple_of(t * tile, tile), tile)
+        down_grad = contract(act[:, cols], gdn[...], 0, 0).astype(BF16)
+        up_grad = contract(hid[:, cols], gup[...], 0, 0).astype(BF16)
+        for piece in range(2):
+            of = slice(piece * half_tile, (piece + 1) * half_tile)
+            d_down_ref[2 * t + piece] = down_grad[of]
+            d_up_ref[2 * t + piece] = up_grad[of]
+
+    for o, (z, a) in enumerate(others):
+        source = z * n_x + a
+        pltpu.make_async_remote_copy(
+            heads_out.at[source], heads_back.at[source], back_send.at[o], back_recv.at[source],
+            device_id=twin, device_id_type=MESH).wait_recv()
+    for k in range(n_ctx * n_x):
+        for h in range(owners):
+            owner = core if h == 0 else 1 - core
+            at = pl.multiple_of((2 * k + owner) * 2 * packed, 2 * packed)
+            for t in range(slots):
+                block = heads_back[k, h, t]
+                ghead_ref[t, pl.ds(at, packed), :] = block[:, :HD]
+                ghead_ref[t, pl.ds(at + packed, packed), :] = block[:, HD:]
     end_lane()
-    for copy in started + pushes:
+    for copy in started + pushes + returns:
         copy.wait_send()
-    for copy in out_copies + late_copies:
-        copy.wait()
 
 
 def layer(sent, tokens, w_out, up, down, vectors, grad_full, lane_shard):
@@ -1187,6 +1218,7 @@
     rows, width = tokens.shape
     hidden = up.shape[1]
     lane = w_out.shape[0]
+    slots = sent.shape[2]
     vmem = pl.BlockSpec(memory_space=pltpu.VMEM)
     anywhere = pl.BlockSpec(memory_space=pl.ANY)
     dma = pltpu.SemaphoreType.DMA
@@ -1203,18 +1235,16 @@
     return pl.pallas_call(
         partial(layer_kernel, n_ctx=n_ctx, n_x=n_x),
         in_specs=[vmem] * 8,
-        out_specs=[vmem] * 6 + [anywhere] * 5,
+        out_specs=[vmem] * 8 + [anywhere],
         out_shape=[
             shape(2 * rows, lane),
             shape(rows, width),
             shape(rows, width, dtype=F32),
-            shape(2 * rows, lane),
+            shape(slots, 2 * chips * (rows // slots), HD),
             shape(2 * rows, width),
             shape(8, width, dtype=F32),
-            shape(4 * rows, hidden),
-            shape(4 * rows, width),
-            shape(4 * rows, width),
-            shape(4 * rows, hidden),
+            shape(chips, hidden // chips, width),
+            shape(chips, width // chips, hidden),
             shape(chips, *lane_shard.shape),
         ],
         scratch_shapes=[
@@ -1240,6 +1270,11 @@
             dma((5,)),
             dma((3, chips)),
             dma((chips,)),
+            low(*sent.shape),
+            dma((chips - 1,)),
+            dma((chips,)),
+            low(2 * rows, lane),
+            low(*sent.shape),
             low(*sent.shape),
             dma((chips - 1,)),
             dma((chips,)),
@@ -1360,19 +1395,15 @@
         merged,
         out_low,
         grad_one,
-        grad_merged,
+        grad_heads,
         grad_att,
         vector_grads,
-        active,
-        hidden_low,
-        grad_down,
-        grad_up,
+        d_down,
+        d_up,
         qkv_lane,
     ) = layer(
         send, tokens.reshape(rows, width), out_lane, up, down, vectors, grad_full, qkv_chip
     )
-    d_down = contract(active, grad_down, 0, 0).astype(BF16)
-    d_up = contract(hidden_low, grad_up, 0, 0).astype(BF16)
     embeds = mm(out_low, proj_full).astype(BF16)
     d_proj = contract(out_low, grad_emb, 0, 0)
     (
@@ -1384,14 +1415,6 @@
         d_gain_two,
         d_shift_two,
     ) = (vector_grads[i] for i in range(7))
-    grad_merged = grad_merged.reshape(2, slots, part, n_lane, HD).transpose(3, 0, 1, 2, 4)
-    grad_heads = lax.all_to_all(grad_merged, LANE, 0, 0, tiled=True)
-
-    def core_order(value):
-        return jnp.where(core == 0, value, jnp.flip(value, axis=1))
-
-    grad_heads = core_order(grad_heads).transpose(2, 0, 1, 3, 4).reshape(slots, seq, HD)
-
     d_out = contract(merged, grad_att, 0, 0).astype(BF16)
 
     spread = (
@@ -1427,8 +1450,8 @@
         all_tokens,
         cos_wide,
         sin_wide,
-        d_down.reshape(n_lane, 2 * shard, width),
-        d_up.reshape(n_lane, 2 * shard, width),
+        d_down,
+        d_up,
         d_out.reshape(n_lane, shard, width),
         small_grad.astype(BF16),
         part,

time: 432 us -> 423 us (0.979)
  matrix products: 16.2 us -> 6.39 us
  Pallas kernels: 364 us -> 370 us
    dot_general x5 -> x3, matrix products: 14.2 us -> 4.37 us  [contract(): lax.dot_general(left, right, (((left_dim,), (right_dim,)), ((), ())), pre...]
  transfers between devices with their start and end apart: 3 -> 2, of which waited for: 1 -> 0; matrix products, arithmetic and copies ran while one was open for 8% -> 5% of each run, Pallas kernels for 17% -> 17%
where the time goes in v2:
time: 423 us; the launch traced here: 420 us
  Pallas kernels  370 us (87%)
  local copies, waits for them, and re-layouts  31.9 us (8%)
  other arithmetic  9.77 us (2%)
  matrix products  6.39 us (2%)
    pallas_call x1, Pallas kernels, layer(): pl.pallas_call(partial(layer_kernel, n_ctx=n_ctx, n_x=n_x), in_specs=[vme...  93.4 us
    pallas_call x1, Pallas kernels, grads(): pl.pallas_call(partial(grads_kernel, n_ctx=n_ctx, n_x=n_x, part=part), in...  77.8 us
    pallas_call x1, Pallas kernels, gather_start(): pl.pallas_call(partial(start_kernel, n_ctx=n_ctx, n_x=n_x), in_specs=[vme...  73.2 us
    pallas_call x1, Pallas kernels, heads(): pl.pallas_call(partial(heads_kernel, n_ctx=n_ctx, n_x=n_x, part=part), in...  67 us
    pallas_call x1, Pallas kernels, finish_grads(): pl.pallas_call(partial(finish_kernel, n_ctx=n_ctx, n_x=n_x), in_specs=[vm...  59 us
  transfers between devices with their start and end apart: 2, of which 0 were waited for; matrix products, arithmetic and copies ran while one was open for 5% of the time, Pallas kernels for 17%

profile of v2, /device:TPU:0, one launch (start us, length us, event | category | flops | bytes accessed | tf_op | source)
XLA Modules:
  0.0 420.2 jit_solution(4181289299738075816)
XLA Ops:
  0.7 1.5 reshape.290
  2.4 0.7 copy.108
  4.2 1.6 constant_dynamic-slice_fusion.1
  5.9 0.8 copy.105
  6.7 0.5 iota_compare_fusion
  7.2 0.6 fusion.12
  7.8 0.6 broadcast_compare_fusion
  8.4 0.5 negate_power_fusion
  9.6 0.8 copy.76
  10.4 1.1 copy.77.head_ref
  11.6 0.6 pad_maximum_fusion.1.small_ref
  12.2 73.2 %gather_start.1 = (bf16[2,2048,1024]{2,1,0:T(8,128)(2,1)}, bf16[16,64,192]{2,1,0:T(8,128)(2,1)}, bf16[16,80,128]{2,1,0:T(8,128)(2,1)}) custom-call(bf16[2,128,1024]{2,1,0:T(8,128)(2,1)} %tok_ref.1, bf16[16,64,192]{2,1,0:T(8,128)(2,1)} %copy.77.head_ref, bf16[80,128]{1,0:T(8,128)(2,1)} %pad_maximum_fusion.1.small_ref), custom_call_target="tpu_custom_call" | custom-call | bytes 8388608 | tf_op jit(solution)/shard_map/gather_start/pallas_call | solution.py:213
  85.4 0.9 slice_convert_fusion
  86.3 1.0 slice.93
  87.6 1.0 multiply_sine_fusion
  88.9 2.4 convolution_add_fusion.full_ref
  91.4 1.3 copy.80.sin_ref
  92.9 1.3 copy.79.cos_ref
  94.7 0.6 reshape.289.b_ref
  95.4 0.7 stack.35.vec_ref
  96.1 0.7 dynamic-slice_bitcast_fusion.wd_ref
  96.8 1.5 fusion
  98.8 1.5 reshape.311.lane_ref
  100.3 0.9 dynamic-slice_bitcast_fusion.1
  101.3 0.8 copy.107
  102.0 67.0 %heads.1 = (bf16[2,2048,64]{2,1,0:T(8,128)(2,1)}, bf16[2,2048,64]{2,1,0:T(8,128)(2,1)}, bf16[2,2048,64]{2,1,0:T(8,128)(2,1)}, f32[2,2048,64]{2,1,0:T(8,128)}, bf...) custom-call(s32[2]{0:T(128)} %len_ref.3, ...), custom_call_target="tpu_custom_call" | custom-call | flops 8589934592 | bytes 8388608 | tf_op jit(solution)/shard_map/heads/pallas_call | solution.py:662
  169.1 93.4 %layer.1 = (bf16[512,512]{1,0:T(8,128)(2,1)}, bf16[256,1024]{1,0:T(8,128)(2,1)}, f32[256,1024]{1,0:T(8,128)}, bf16[2,2048,64]{2,1,0:T(8,128)(2,1)}, bf16[512,102...) custom-call(bf16[8,2,2,64,128]{4,3,2,1,0:T(8,128)(2,1)} %get-tuple-e, ...), custom_call_target="tpu_custom_call" | custom-call | flops 4294967296 | bytes 4194304 | tf_op jit(solution)/shard_map/layer/pallas_call | solution.py:1235
  262.5 0.8 slice.97
  263.3 0.8 convert.34
  264.0 2.0 convolution_convert_fusion.2
  266.1 1.8 multiply_reduce_fusion
  268.0 0.6 reshape.301.dot_ref
  269.8 0.7 pad_maximum_fusion.small_ref
  270.6 1.7 convolution_convert_fusion
  272.3 77.8 %grads.1 = (bf16[8,2,2,64,384]{4,3,2,1,0:T(8,128)(2,1)}, bf16[16,80,192]{2,1,0:T(8,128)(2,1)}, bf16[256,1024]{1,0:T(8,128)(2,1)}, bf16[64,1024]{1,0:T(8,128)(2,1)}, bf16[80,128]{1,0:T(8,128)(2,1)}) custom-call(s32[2]{0:T(128)} %len_ref.3, bf16[2,2048,64]{2,1,0:T(8,128)(2,1)} %get-tuple-element.57.q_ref, bf16[2,2048,64]{2,1,0:T(8,128)(2,1)} %get-tuple-element.58.k_ref, ...), custom_call_target="tpu_custom_call" | custom-call | flops 21474836480 | bytes 16777216 | tf_op jit(solution)/shard_map/grads/pallas_call | solution.py:892
  350.1 59.0 %finish_grads.1 = (f32[256,1024]{1,0:T(8,128)}, f32[64,4096]{1,0:T(8,128)}, f32[64,1024]{1,0:T(8,128)}, f32[80,128]{1,0:T(8,128)}, f32[64,3072]{1,0:T(8,128)}, /...) custom-call(bf16[64,1024]{1,0:T(8,128)(2,1)} %get-tuple-element.68.out_ref, bf16[80,128]{1,0:T(8,128)(2,1)} %get-tuple-element.69.small_ref, ...), custom_call_target="tpu_custom_call" | custom-call | bytes 12582912 | tf_op jit(solution)/shard_map/finish_grads/pallas_call | solution.py:376
  409.1 0.8 slice_bitcast_fusion
  409.9 1.4 slice.109
  411.3 0.6 slice.127
  411.9 0.6 fusion.3
  412.5 0.8 reshape.305
  413.4 0.6 dynamic_slice.44
  414.0 0.8 copy.118
  414.8 1.9 copy.119
  416.7 0.9 copy.120
  417.6 0.7 copy.121
  418.3 1.0 copy.122
  419.3 1.0 copy.123
  (104 shorter events, 5.2 us)
Async XLA Ops:
  0.6 95.4 %copy-start = (bf16[256,1024]{1,0:T(8,128)(2,1)S(1)}, bf16[256,1024]{1,0:T(8,128)(2,1)}, u32[]{:S(2)}) copy-start(bf16[256,1024]{1,0:T(8,128)(2,1)} %param.27) | copy-start | bytes 1572868
  0.7 2.9 copy-start.5
  2.2 1.9 copy-start.3
  3.1 97.2 %collective-permute-start = (bf16[64,8,2,128]{3,1,2,0:T(8,128)(2,1)}, bf16[64,8,2,128]{3,1,2,0:T(8,128)(2,1)}, u32[]{:S(2)}, u32[]{:S(2)}) collective-permute-start(bf16[64,8,2,128]{3,1,2,0:T(8,128)(2,1)} %bitcast.76), channel_id=1, source_target_pairs={{0,1},{1,0},{2,3},{3,2},{4,5},{5,4},{6,7},{7,6},{8,9},{9,8},{10,11... | collective-permute-start | bytes 786440 | tf_op jit(solution)/shard_map/ppermute | solution.py:34
  4.1 3.1 copy-start.24
  4.1 5.3 %copy-start.16 = (bf16[192]{0:T(256)(128)(2,1)S(1)}, bf16[192]{0:T(256)(128)(2,1)}, u32[]{:S(2)}) copy-start(bf16[192]{0:T(256)(128)(2,1)} %param.20) | copy-start | bytes 1156
  4.1 5.3 %copy-start.17 = (bf16[64]{0:T(256)(128)(2,1)S(1)}, bf16[64]{0:T(256)(128)(2,1)}, u32[]{:S(2)}) copy-start(bf16[64]{0:T(256)(128)(2,1)} %param.22) | copy-start | bytes 388
  4.1 5.3 %copy-start.18 = (bf16[64]{0:T(256)(128)(2,1)S(1)}, bf16[64]{0:T(256)(128)(2,1)}, u32[]{:S(2)}) copy-start(bf16[64]{0:T(256)(128)(2,1)} %param.23) | copy-start | bytes 388
  4.2 5.3 %copy-start.19 = (bf16[64]{0:T(256)(128)(2,1)S(1)}, bf16[64]{0:T(256)(128)(2,1)}, u32[]{:S(2)}) copy-start(bf16[64]{0:T(256)(128)(2,1)} %param.24) | copy-start | bytes 388
  4.2 5.3 %copy-start.20 = (bf16[256]{0:T(256)(128)(2,1)S(1)}, bf16[256]{0:T(256)(128)(2,1)}, u32[]{:S(2)}) copy-start(bf16[256]{0:T(256)(128)(2,1)} %param.26) | copy-start | bytes 1540
  4.2 5.3 %copy-start.21 = (bf16[64]{0:T(256)(128)(2,1)S(1)}, bf16[64]{0:T(256)(128)(2,1)}, u32[]{:S(2)}) copy-start(bf16[64]{0:T(256)(128)(2,1)} %param.28) | copy-start | bytes 388
  4.2 5.2 %copy-start.22 = (bf16[64]{0:T(256)(128)(2,1)S(1)}, bf16[64]{0:T(256)(128)(2,1)}, u32[]{:S(2)}) copy-start(bf16[64]{0:T(256)(128)(2,1)} %param.29) | copy-start | bytes 388
  4.2 5.2 %copy-start.23 = (bf16[64]{0:T(256)(128)(2,1)S(1)}, bf16[64]{0:T(256)(128)(2,1)}, u32[]{:S(2)}) copy-start(bf16[64]{0:T(256)(128)(2,1)} %param.30) | copy-start | bytes 388
  6.7 4.9 %copy-start.11 = (bf16[64,128]{1,0:T(8,128)(2,1)S(1)}, bf16[64,128]{1,0:T(8,128)(2,1)}, u32[]{:S(2)}) copy-start(bf16[64,128]{1,0:T(8,128)(2,1)} %param.31) | copy-start | bytes 49156
  6.7 90.1 %collective-permute-start.1 = (bf16[64,3,8,64]{3,2,1,0:T(8,128)(2,1)}, bf16[64,3,8,64]{3,2,1,0:T(8,128)(2,1)}, u32[]{:S(2)}, u32[]{:S(2)}) collective-permute-start(bf16[64,3,8,64]{3,2,1,0:T(8,128)(2,1)} %bitcast.73), channel_id=1, source_target_pairs={{0,1},{1,0},{2,3},{3,2},{4,5},{5,4},{6,7},{7,6},{8,9},{9,8},{10,11... | collective-permute-start | bytes 589832 | tf_op jit(solution)/shard_map/ppermute | solution.py:34
  10.4 77.0 %copy-start.12 = (pred[2]{0:T(512)(128)(4,1)S(1)}, pred[2]{0:T(512)(128)(4,1)}, u32[]{:S(2)}) copy-start(pred[2]{0:T(512)(128)(4,1)} %get-tuple-element.105) | copy-start | bytes 10
  10.4 77.1 %copy-start.10 = (bf16[2,128,128]{2,1,0:T(8,128)(2,1)S(1)}, bf16[2,128,128]{2,1,0:T(8,128)(2,1)}, u32[]{:S(2)}) copy-start(bf16[2,128,128]{2,1,0:T(8,128)(2,1)} %param.33) | copy-start | bytes 196612
  10.4 77.1 %copy-start.15 = (pred[2,128]{1,0:T(4,128)(4,1)S(1)}, pred[2,128]{1,0:T(4,128)(4,1)}, u32[]{:S(2)}) copy-start(pred[2,128]{1,0:T(4,128)(4,1)} %broadcast_compare_fusion) | copy-start | bytes 772
  10.4 77.2 %copy-start.14 = (f32[32]{0:T(128)S(1)}, f32[32]{0:T(128)}, u32[]{:S(2)}) copy-start(f32[32]{0:T(128)} %negate_power_fusion) | copy-start | bytes 388
  10.4 78.2 %copy-start.4 = (bf16[64,8,2,2,128]{4,3,2,1,0:T(2,128)(2,1)S(1)}, bf16[64,8,2,2,128]{4,3,2,1,0:T(2,128)(2,1)}, u32[]{:S(2)}) copy-start(bf16[64,8,2,2,128]{4,3,2,1,0:T(2,128)(2,1)} %copy-done.3) | copy-start | bytes 1572868
  10.4 78.5 %copy-start.13 = (pred[256]{0:T(512)(128)(4,1)S(1)}, pred[256]{0:T(512)(128)(4,1)}, u32[]{:S(2)}) copy-start(pred[256]{0:T(512)(128)(4,1)} %fusion.12) | copy-start | bytes 772
  169.1 97.0 %copy-start.2 = (f32[2,2048,64]{2,1,0:T(8,128)S(1)}, f32[2,2048,64]{2,1,0:T(8,128)}, u32[]{:S(2)}) copy-start(f32[2,2048,64]{2,1,0:T(8,128)} %get-tuple-element.62) | copy-start | bytes 3145732
  264.0 5.3 %copy-start.1 = (bf16[256,1024]{1,0:T(8,128)(2,1)S(1)}, bf16[256,1024]{1,0:T(8,128)(2,1)}, u32[]{:S(2)}) copy-start(bf16[256,1024]{1,0:T(8,128)(2,1)} %get-tuple-element.56) | copy-start | bytes 1572868
  267.9 2.7 copy-start.25
  267.9 2.6 copy-start.26
  409.1 7.6 %copy-start.8 = (f32[64,3072]{1,0:T(8,128)S(1)}, f32[64,3072]{1,0:T(8,128)}, u32[]{:S(2)}) copy-start(f32[64,3072]{1,0:T(8,128)} %get-tuple-element.125) | copy-start | bytes 2359300
  409.1 8.5 %copy-start.9 = (f32[64,1024]{1,0:T(8,128)S(1)}, f32[64,1024]{1,0:T(8,128)}, u32[]{:S(2)}) copy-start(f32[64,1024]{1,0:T(8,128)} %get-tuple-element.127) | copy-start | bytes 786436
  414.0 4.3 %copy-start.7 = (f32[64,4096]{1,0:T(8,128)S(1)}, f32[64,4096]{1,0:T(8,128)}, u32[]{:S(2)}) copy-start(f32[64,4096]{1,0:T(8,128)} %get-tuple-element.131) | copy-start | bytes 3145732
  416.7 2.6 copy-start.6

commit v3 on v2

--- a/solution.py
+++ b/solution.py
@@ -293,8 +293,7 @@
     qkvs[me] = sum_qkv[me]
 
     def add_head(source, rows_of, first):
-        weight = jnp.concatenate(
-            [weight_ref[b, source] for b in range(weight_ref.shape[0])], axis=0)
+        weight = weight_ref[source]
         for h in range(2):
             owner = core if h == 0 else 1 - core
             rows = rows_of(owner)
@@ -1377,12 +1376,6 @@
     bias_lane = pick(up_bias.reshape(n_lane, 2, 2, ff_half), core, 1)
     up_bias_own = pick(bias_lane, slot, 1).reshape(-1)
 
-    qkv_split = w_qkv.reshape(shard, 3, n_lane, 2, HD)
-    qkv_mine = pick(qkv_split, core, 3)
-    qkv_theirs = swap_core(pick(qkv_split, 1 - core, 3))
-    qkv_chip = two_lanes(qkv_mine, qkv_theirs).transpose(3, 0, 1, 2, 4)
-    qkv_chip = qkv_chip.reshape(n_lane, 2 * shard, head_cols)
-
     place = me * part + jnp.arange(part, dtype=jnp.int32)
     live = (place[None, :] < lengths[:, None]).reshape(rows, 1)
     grad_out = jnp.where(live, cot_out.reshape(rows, width).astype(F32), 0.0)
@@ -1402,7 +1395,7 @@
         d_up,
         qkv_lane,
     ) = layer(
-        send, tokens.reshape(rows, width), out_lane, up, down, vectors, grad_full, qkv_chip
+        send, tokens.reshape(rows, width), out_lane, up, down, vectors, grad_full, head_weight
     )
     embeds = mm(out_low, proj_full).astype(BF16)
     d_proj = contract(out_low, grad_emb, 0, 0)

time: 423 us -> 411 us (0.972)
  local copies, waits for them, and re-layouts: 31.9 us -> 25.2 us
  transfers between devices with their start and end apart: 2 -> 1, of which waited for: 0 -> 0; matrix products, arithmetic and copies ran while one was open for 5% -> 3% of each run, Pallas kernels for 17% -> 18%
where the time goes in v3:
time: 411 us; the launch traced here: 409 us
  Pallas kernels  370 us (90%)
  local copies, waits for them, and re-layouts  25.2 us (6%)
  other arithmetic  6.25 us (2%)
  matrix products  5.36 us (1%)
    pallas_call x1, Pallas kernels, layer(): pl.pallas_call(partial(layer_kernel, n_ctx=n_ctx, n_x=n_x), in_specs=[vme...  93.4 us
    pallas_call x1, Pallas kernels, grads(): pl.pallas_call(partial(grads_kernel, n_ctx=n_ctx, n_x=n_x, part=part), in...  77.7 us
    pallas_call x1, Pallas kernels, gather_start(): pl.pallas_call(partial(start_kernel, n_ctx=n_ctx, n_x=n_x), in_specs=[vme...  72.9 us
    pallas_call x1, Pallas kernels, heads(): pl.pallas_call(partial(heads_kernel, n_ctx=n_ctx, n_x=n_x, part=part), in...  67 us
    pallas_call x1, Pallas kernels, finish_grads(): pl.pallas_call(partial(finish_kernel, n_ctx=n_ctx, n_x=n_x), in_specs=[vm...  59.2 us
  transfers between devices with their start and end apart: 1, of which 0 were waited for; matrix products, arithmetic and copies ran while one was open for 3% of the time, Pallas kernels for 18%

profile of v3, /device:TPU:0, one launch (start us, length us, event | category | flops | bytes accessed | tf_op | source)
XLA Modules:
  0.0 408.8 jit_solution(11113628511620441315)
XLA Ops:
  0.8 1.5 reshape.283
  2.3 0.2 constant_dynamic-slice_fusion
  2.5 0.6 collective-permute-start
  3.5 0.5 reshape.277
  3.9 0.8 copy.47
  4.7 1.1 copy.48.head_ref
  5.9 0.6 pad_maximum_fusion.1.small_ref
  6.5 72.9 %gather_start.1 = (bf16[2,2048,1024]{2,1,0:T(8,128)(2,1)}, bf16[16,64,192]{2,1,0:T(8,128)(2,1)}, bf16[16,80,128]{2,1,0:T(8,128)(2,1)}) custom-call(bf16[2,128,1024]{2,1,0:T(8,128)(2,1)} %tok_ref.1, bf16[16,64,192]{2,1,0:T(8,128)(2,1)} %copy.48.head_ref, bf16[80,128]{1,0:T(8,128)(2,1)} %pad_maximum_fusion.1.small_ref), custom_call_target="tpu_custom_call" | custom-call | bytes 8388608 | tf_op jit(solution)/shard_map/gather_start/pallas_call | solution.py:213
  79.3 0.9 slice_convert_fusion
  80.2 1.0 slice.93
  81.3 0.7 dynamic-slice_bitcast_fusion.wd_ref
  82.1 0.3 constant_dynamic-slice_fusion.1
  82.4 1.0 multiply_sine_fusion
  83.4 0.1 tile.28
  83.5 1.3 copy.51.sin_ref
  84.8 0.1 tile.26
  84.9 1.3 copy.50.cos_ref
  86.8 0.6 reshape.282.b_ref
  87.5 0.1 broadcast_select_fusion
  87.6 0.7 stack.21.vec_ref
  88.3 1.3 convolution_add_fusion.full_ref
  89.7 0.8 copy.68
  90.4 67.0 %heads.1 = (bf16[2,2048,64]{2,1,0:T(8,128)(2,1)}, bf16[2,2048,64]{2,1,0:T(8,128)(2,1)}, bf16[2,2048,64]{2,1,0:T(8,128)(2,1)}, f32[2,2048,64]{2,1,0:T(8,128)}, bf...) custom-call(s32[2]{0:T(128)} %len_ref.3, ...), custom_call_target="tpu_custom_call" | custom-call | flops 8589934592 | bytes 8388608 | tf_op jit(solution)/shard_map/heads/pallas_call | solution.py:661
  157.5 93.4 %layer.1 = (bf16[512,512]{1,0:T(8,128)(2,1)}, bf16[256,1024]{1,0:T(8,128)(2,1)}, f32[256,1024]{1,0:T(8,128)}, bf16[2,2048,64]{2,1,0:T(8,128)(2,1)}, bf16[512,102...) custom-call(bf16[8,2,2,64,128]{4,3,2,1,0:T(8,128)(2,1)} %get-tuple-e, ...), custom_call_target="tpu_custom_call" | custom-call | flops 4294967296 | bytes 4194304 | tf_op jit(solution)/shard_map/layer/pallas_call | solution.py:1234
  250.9 0.8 slice.97
  251.7 0.8 convert.34
  252.4 2.0 convolution_convert_fusion.2
  254.5 1.8 multiply_reduce_fusion
  256.3 0.6 reshape.292.dot_ref
  257.6 0.1 concatenate.16
  257.7 0.2 copy.53
  257.9 0.3 convolution_convert_fusion.1
  258.2 0.7 pad_maximum_fusion.small_ref
  259.0 1.7 convolution_convert_fusion
  260.7 77.7 %grads.1 = (bf16[8,2,2,64,384]{4,3,2,1,0:T(8,128)(2,1)}, bf16[16,80,192]{2,1,0:T(8,128)(2,1)}, bf16[256,1024]{1,0:T(8,128)(2,1)}, bf16[64,1024]{1,0:T(8,128)(2,1)}, bf16[80,128]{1,0:T(8,128)(2,1)}) custom-call(s32[2]{0:T(128)} %len_ref.3, bf16[2,2048,64]{2,1,0:T(8,128)(2,1)} %get-tuple-element.57.q_ref, bf16[2,2048,64]{2,1,0:T(8,128)(2,1)} %get-tuple-element.58.k_ref, ...), custom_call_target="tpu_custom_call" | custom-call | flops 21474836480 | bytes 16777216 | tf_op jit(solution)/shard_map/grads/pallas_call | solution.py:891
  338.4 59.2 %finish_grads.1 = (f32[256,1024]{1,0:T(8,128)}, f32[64,4096]{1,0:T(8,128)}, f32[64,1024]{1,0:T(8,128)}, f32[80,128]{1,0:T(8,128)}, f32[64,3072]{1,0:T(8,128)}, /...) custom-call(bf16[64,1024]{1,0:T(8,128)(2,1)} %get-tuple-element.68.out_ref, bf16[80,128]{1,0:T(8,128)(2,1)} %get-tuple-element.69.small_ref, ...), custom_call_target="tpu_custom_call" | custom-call | bytes 12582912 | tf_op jit(solution)/shard_map/finish_grads/pallas_call | solution.py:375
  397.7 0.8 slice_bitcast_fusion
  398.4 1.4 slice.109
  399.8 0.6 slice.127
  400.4 0.6 fusion.1
  401.0 0.8 reshape.296
  401.9 0.6 dynamic_slice.35
  402.6 0.8 copy.79
  403.3 1.9 copy.80
  405.2 0.9 copy.81
  406.1 0.7 copy.82
  406.8 1.0 copy.83
  407.8 1.0 copy.84
  (85 shorter events, 2.0 us)
Async XLA Ops:
  0.7 80.7 %copy-start = (bf16[256,1024]{1,0:T(8,128)(2,1)S(1)}, bf16[256,1024]{1,0:T(8,128)(2,1)}, u32[]{:S(2)}) copy-start(bf16[256,1024]{1,0:T(8,128)(2,1)} %param.27) | copy-start | bytes 1572868
  0.7 2.4 copy-start.19
  0.7 2.6 copy-start.18
  0.7 2.6 copy-start.17
  0.7 2.6 copy-start.16
  0.7 2.6 copy-start.15
  0.7 2.6 copy-start.14
  0.7 2.6 copy-start.13
  0.7 2.6 copy-start.12
  0.7 2.6 copy-start.11
  0.8 2.7 copy-start.7
  2.5 3.4 copy-start.10
  2.5 87.1 %collective-permute-start = (bf16[64,8,2,128]{3,1,2,0:T(8,128)(2,1)S(1)}, bf16[64,8,2,128]{3,1,2,0:T(8,128)(2,1)S(1)}, u32[]{:S(2)}, u32[]{:S(2)}) collective-permute-start(bf16[64,8,2,128]{3,1,2,0:T(8,128)(2,1)S(1)} %bitcast.92), channel_id=1, source_target_pairs={{0,1},{1,0},{2,3},{3,2},{4,5},{5,4},{6,7},{7,6},{8,9},{9,8},{10,11... | collective-permute-start | bytes 786440 | tf_op jit(solution)/shard_map/ppermute | solution.py:34
  84.8 2.7 copy-start.9
  84.8 3.5 copy-start.6
  157.5 97.0 %copy-start.2 = (f32[2,2048,64]{2,1,0:T(8,128)S(1)}, f32[2,2048,64]{2,1,0:T(8,128)}, u32[]{:S(2)}) copy-start(f32[2,2048,64]{2,1,0:T(8,128)} %get-tuple-element.62) | copy-start | bytes 3145732
  252.4 5.3 %copy-start.1 = (bf16[256,1024]{1,0:T(8,128)(2,1)S(1)}, bf16[256,1024]{1,0:T(8,128)(2,1)}, u32[]{:S(2)}) copy-start(bf16[256,1024]{1,0:T(8,128)(2,1)} %get-tuple-element.56) | copy-start | bytes 1572868
  256.3 2.7 copy-start.20
  256.3 2.7 copy-start.21
  397.6 7.6 %copy-start.5 = (f32[64,3072]{1,0:T(8,128)S(1)}, f32[64,3072]{1,0:T(8,128)}, u32[]{:S(2)}) copy-start(f32[64,3072]{1,0:T(8,128)} %get-tuple-element.123) | copy-start | bytes 2359300
  397.6 8.5 %copy-start.8 = (f32[64,1024]{1,0:T(8,128)S(1)}, f32[64,1024]{1,0:T(8,128)}, u32[]{:S(2)}) copy-start(f32[64,1024]{1,0:T(8,128)} %get-tuple-element.125) | copy-start | bytes 786436
  402.6 4.3 %copy-start.4 = (f32[64,4096]{1,0:T(8,128)S(1)}, f32[64,4096]{1,0:T(8,128)}, u32[]{:S(2)}) copy-start(f32[64,4096]{1,0:T(8,128)} %get-tuple-element.129) | copy-start | bytes 3145732
  405.2 2.6 copy-start.3

commit v4 on v3

--- a/solution.py
+++ b/solution.py
@@ -990,7 +990,6 @@
     heads_in[chip] = sent_ref[chip]
     begin_lane, relay_lane, end_lane = lane_gather(
         lane_ref, lanes_out, lane_send, lane_recv, out_sem.at[0], n_ctx, n_x)
-    begin_lane()
     rows, width = tok_ref.shape
     half = rows // 2
     tile = 256
@@ -1050,6 +1049,7 @@
         pltpu.make_async_remote_copy(
             sent_ref.at[source], heads_in.at[source], push_send.at[o], push_recv.at[source],
             device_id=twin, device_id_type=MESH).wait_recv()
+    begin_lane()
     _, owners, slots, packed, pair_width = heads_in.shape
     for k in range(0, n_ctx * n_x, 2):
         for h in range(owners):

time: 411 us -> 411 us (level)
  no operation moved by 1% of the time
where the time goes in v4:
time: 411 us; the launch traced here: 409 us
  Pallas kernels  370 us (90%)
  local copies, waits for them, and re-layouts  25.2 us (6%)
  other arithmetic  6.25 us (2%)
  matrix products  5.36 us (1%)
    pallas_call x1, Pallas kernels, layer(): pl.pallas_call(partial(layer_kernel, n_ctx=n_ctx, n_x=n_x), in_specs=[vme...  92.9 us
    pallas_call x1, Pallas kernels, grads(): pl.pallas_call(partial(grads_kernel, n_ctx=n_ctx, n_x=n_x, part=part), in...  78.3 us
    pallas_call x1, Pallas kernels, gather_start(): pl.pallas_call(partial(start_kernel, n_ctx=n_ctx, n_x=n_x), in_specs=[vme...  72.9 us
    pallas_call x1, Pallas kernels, heads(): pl.pallas_call(partial(heads_kernel, n_ctx=n_ctx, n_x=n_x, part=part), in...  67 us
    pallas_call x1, Pallas kernels, finish_grads(): pl.pallas_call(partial(finish_kernel, n_ctx=n_ctx, n_x=n_x), in_specs=[vm...  59.2 us
  transfers between devices with their start and end apart: 1, of which 0 were waited for; matrix products, arithmetic and copies ran while one was open for 3% of the time, Pallas kernels for 18%

profile of v4, /device:TPU:0, one launch (start us, length us, event | category | flops | bytes accessed | tf_op | source)
XLA Modules:
  0.0 408.7 jit_solution(5386133970524134275)
XLA Ops:
  0.8 1.5 reshape.283
  2.3 0.2 constant_dynamic-slice_fusion
  2.5 0.6 collective-permute-start
  3.5 0.5 reshape.277
  3.9 0.8 copy.47
  4.7 1.1 copy.48.head_ref
  5.9 0.6 pad_maximum_fusion.1.small_ref
  6.5 72.9 %gather_start.1 = (bf16[2,2048,1024]{2,1,0:T(8,128)(2,1)}, bf16[16,64,192]{2,1,0:T(8,128)(2,1)}, bf16[16,80,128]{2,1,0:T(8,128)(2,1)}) custom-call(bf16[2,128,1024]{2,1,0:T(8,128)(2,1)} %tok_ref.1, bf16[16,64,192]{2,1,0:T(8,128)(2,1)} %copy.48.head_ref, bf16[80,128]{1,0:T(8,128)(2,1)} %pad_maximum_fusion.1.small_ref), custom_call_target="tpu_custom_call" | custom-call | bytes 8388608 | tf_op jit(solution)/shard_map/gather_start/pallas_call | solution.py:213
  79.3 0.9 slice_convert_fusion
  80.2 1.0 slice.93
  81.3 0.7 dynamic-slice_bitcast_fusion.wd_ref
  82.1 0.3 constant_dynamic-slice_fusion.1
  82.4 1.0 multiply_sine_fusion
  83.4 0.1 tile.28
  83.5 1.3 copy.51.sin_ref
  84.8 0.1 tile.26
  84.9 1.3 copy.50.cos_ref
  86.8 0.6 reshape.282.b_ref
  87.5 0.1 broadcast_select_fusion
  87.6 0.7 stack.21.vec_ref
  88.3 1.3 convolution_add_fusion.full_ref
  89.7 0.8 copy.68
  90.4 67.0 %heads.1 = (bf16[2,2048,64]{2,1,0:T(8,128)(2,1)}, bf16[2,2048,64]{2,1,0:T(8,128)(2,1)}, bf16[2,2048,64]{2,1,0:T(8,128)(2,1)}, f32[2,2048,64]{2,1,0:T(8,128)}, bf...) custom-call(s32[2]{0:T(128)} %len_ref.3, ...), custom_call_target="tpu_custom_call" | custom-call | flops 8589934592 | bytes 8388608 | tf_op jit(solution)/shard_map/heads/pallas_call | solution.py:661
  157.5 92.9 %layer.1 = (bf16[512,512]{1,0:T(8,128)(2,1)}, bf16[256,1024]{1,0:T(8,128)(2,1)}, f32[256,1024]{1,0:T(8,128)}, bf16[2,2048,64]{2,1,0:T(8,128)(2,1)}, bf16[512,102...) custom-call(bf16[8,2,2,64,128]{4,3,2,1,0:T(8,128)(2,1)} %get-tuple-e, ...), custom_call_target="tpu_custom_call" | custom-call | flops 4294967296 | bytes 4194304 | tf_op jit(solution)/shard_map/layer/pallas_call | solution.py:1234
  250.4 0.8 slice.97
  251.1 0.8 convert.34
  251.9 2.0 convolution_convert_fusion.2
  253.9 1.8 multiply_reduce_fusion
  255.8 0.6 reshape.292.dot_ref
  257.1 0.1 concatenate.16
  257.2 0.2 copy.53
  257.4 0.3 convolution_convert_fusion.1
  257.7 0.7 pad_maximum_fusion.small_ref
  258.4 1.7 convolution_convert_fusion
  260.1 78.3 %grads.1 = (bf16[8,2,2,64,384]{4,3,2,1,0:T(8,128)(2,1)}, bf16[16,80,192]{2,1,0:T(8,128)(2,1)}, bf16[256,1024]{1,0:T(8,128)(2,1)}, bf16[64,1024]{1,0:T(8,128)(2,1)}, bf16[80,128]{1,0:T(8,128)(2,1)}) custom-call(s32[2]{0:T(128)} %len_ref.3, bf16[2,2048,64]{2,1,0:T(8,128)(2,1)} %get-tuple-element.57.q_ref, bf16[2,2048,64]{2,1,0:T(8,128)(2,1)} %get-tuple-element.58.k_ref, ...), custom_call_target="tpu_custom_call" | custom-call | flops 21474836480 | bytes 16777216 | tf_op jit(solution)/shard_map/grads/pallas_call | solution.py:891
  338.4 59.2 %finish_grads.1 = (f32[256,1024]{1,0:T(8,128)}, f32[64,4096]{1,0:T(8,128)}, f32[64,1024]{1,0:T(8,128)}, f32[80,128]{1,0:T(8,128)}, f32[64,3072]{1,0:T(8,128)}, /...) custom-call(bf16[64,1024]{1,0:T(8,128)(2,1)} %get-tuple-element.68.out_ref, bf16[80,128]{1,0:T(8,128)(2,1)} %get-tuple-element.69.small_ref, ...), custom_call_target="tpu_custom_call" | custom-call | bytes 12582912 | tf_op jit(solution)/shard_map/finish_grads/pallas_call | solution.py:375
  397.6 0.8 slice_bitcast_fusion
  398.4 1.4 slice.109
  399.8 0.6 slice.127
  400.4 0.6 fusion.1
  401.0 0.8 reshape.296
  401.9 0.6 dynamic_slice.35
  402.6 0.8 copy.79
  403.3 1.9 copy.80
  405.2 0.9 copy.81
  406.1 0.7 copy.82
  406.8 1.0 copy.83
  407.8 1.0 copy.84
  (85 shorter events, 2.0 us)
Async XLA Ops:
  0.7 80.7 %copy-start = (bf16[256,1024]{1,0:T(8,128)(2,1)S(1)}, bf16[256,1024]{1,0:T(8,128)(2,1)}, u32[]{:S(2)}) copy-start(bf16[256,1024]{1,0:T(8,128)(2,1)} %param.27) | copy-start | bytes 1572868
  0.7 2.4 copy-start.19
  0.7 2.6 copy-start.18
  0.7 2.6 copy-start.17
  0.7 2.6 copy-start.16
  0.7 2.6 copy-start.15
  0.7 2.6 copy-start.14
  0.7 2.6 copy-start.13
  0.7 2.6 copy-start.12
  0.7 2.6 copy-start.11
  0.8 2.7 copy-start.7
  2.5 3.4 copy-start.10
  2.5 87.1 %collective-permute-start = (bf16[64,8,2,128]{3,1,2,0:T(8,128)(2,1)S(1)}, bf16[64,8,2,128]{3,1,2,0:T(8,128)(2,1)S(1)}, u32[]{:S(2)}, u32[]{:S(2)}) collective-permute-start(bf16[64,8,2,128]{3,1,2,0:T(8,128)(2,1)S(1)} %bitcast.92), channel_id=1, source_target_pairs={{0,1},{1,0},{2,3},{3,2},{4,5},{5,4},{6,7},{7,6},{8,9},{9,8},{10,11... | collective-permute-start | bytes 786440 | tf_op jit(solution)/shard_map/ppermute | solution.py:34
  84.8 2.7 copy-start.9
  84.8 3.5 copy-start.6
  157.5 96.5 %copy-start.2 = (f32[2,2048,64]{2,1,0:T(8,128)S(1)}, f32[2,2048,64]{2,1,0:T(8,128)}, u32[]{:S(2)}) copy-start(f32[2,2048,64]{2,1,0:T(8,128)} %get-tuple-element.62) | copy-start | bytes 3145732
  251.9 5.3 %copy-start.1 = (bf16[256,1024]{1,0:T(8,128)(2,1)S(1)}, bf16[256,1024]{1,0:T(8,128)(2,1)}, u32[]{:S(2)}) copy-start(bf16[256,1024]{1,0:T(8,128)(2,1)} %get-tuple-element.56) | copy-start | bytes 1572868
  255.8 2.7 copy-start.20
  255.8 2.7 copy-start.21
  397.6 7.6 %copy-start.5 = (f32[64,3072]{1,0:T(8,128)S(1)}, f32[64,3072]{1,0:T(8,128)}, u32[]{:S(2)}) copy-start(f32[64,3072]{1,0:T(8,128)} %get-tuple-element.123) | copy-start | bytes 2359300
  397.6 8.5 %copy-start.8 = (f32[64,1024]{1,0:T(8,128)S(1)}, f32[64,1024]{1,0:T(8,128)}, u32[]{:S(2)}) copy-start(f32[64,1024]{1,0:T(8,128)} %get-tuple-element.125) | copy-start | bytes 786436
  402.5 4.3 %copy-start.4 = (f32[64,4096]{1,0:T(8,128)S(1)}, f32[64,4096]{1,0:T(8,128)}, u32[]{:S(2)}) copy-start(f32[64,4096]{1,0:T(8,128)} %get-tuple-element.129) | copy-start | bytes 3145732
  405.2 2.6 copy-start.3
